TPU v7x, 32 devices: a whole 2x2x4 slice. The times are simulated.
32 devices in a mesh: dp: 8 (over y, x, core), fsdp: 4 (over z).
Axes of the slice: x: 2, y: 2, z: 4, core: 2. Of those that a mesh axis runs over, the one named last changes fastest.
Arguments:
- tokens: bfloat16 [32768, 768], P(('dp', 'fsdp')), may hold values from -6 to 6
- cotangent: bfloat16 [32768, 768], P(('dp', 'fsdp')), may hold values from -6 to 6
- doc_lengths: int32 [64, 4], P(('dp', 'fsdp')), may hold values from 1 to 288, 512 in all within a row
- query_ids: int32 [256, 1], P(('dp', 'fsdp')), may hold values from 0 to 63
- qkv_weight: bfloat16 [768, 2304], P(('dp', 'fsdp')), may hold values from -0.21875 to 0.21875
- query_bias: bfloat16 [768], P(('dp', 'fsdp')), may hold values from -3 to 3
- value_bias: bfloat16 [768], P(('dp', 'fsdp')), may hold values from -3 to 3
- attn_weight: bfloat16 [768, 768], P(('dp', 'fsdp')), may hold values from -0.875 to 0.875
- attn_bias: bfloat16 [768], P(('dp', 'fsdp')), may hold values from -2 to 2
- first_gain: bfloat16 [768], P(('dp', 'fsdp')), may hold values from 0.5 to 1.5
- first_shift: bfloat16 [768], P(('dp', 'fsdp')), may hold values from -2 to 2
- inner_weight: bfloat16 [768, 3072], P(('dp', 'fsdp')), may hold values from -0.21875 to 0.21875
- inner_bias: bfloat16 [3072], P(('dp', 'fsdp')), may hold values from -3 to 3
- outer_weight: bfloat16 [3072, 768], P(('dp', 'fsdp')), may hold values from -0.21875 to 0.21875
- outer_bias: bfloat16 [768], P(('dp', 'fsdp')), may hold values from -2 to 2
- second_gain: bfloat16 [768], P(('dp', 'fsdp')), may hold values from 0.5 to 1.5
- second_shift: bfloat16 [768], P(('dp', 'fsdp')), may hold values from -2 to 2
- span_weight: bfloat16 [768, 128], P(('dp', 'fsdp')), may hold values from -0.21875 to 0.21875
- answer_vector: bfloat16 [128], P(('dp', 'fsdp')), may hold values from -1 to 1
Outputs:
- log_likelihood: float32 [], replicated
- layer_output: bfloat16 [32768, 768], P(('dp', 'fsdp'))
- input_grad: float32 [32768, 768], P(('dp', 'fsdp'))
- qkv_weight_grad: float32 [768, 2304], P(('dp', 'fsdp'))
- query_bias_grad: float32 [768], P(('dp', 'fsdp'))
- value_bias_grad: float32 [768], P(('dp', 'fsdp'))
- attn_weight_grad: float32 [768, 768], P(('dp', 'fsdp'))
- attn_bias_grad: float32 [768], P(('dp', 'fsdp'))
- first_gain_grad: float32 [768], P(('dp', 'fsdp'))
- first_shift_grad: float32 [768], P(('dp', 'fsdp'))
- inner_weight_grad: float32 [768, 3072], P(('dp', 'fsdp'))
- inner_bias_grad: float32 [3072], P(('dp', 'fsdp'))
- outer_weight_grad: float32 [3072, 768], P(('dp', 'fsdp'))
- outer_bias_grad: float32 [768], P(('dp', 'fsdp'))
- second_gain_grad: float32 [768], P(('dp', 'fsdp'))
- second_shift_grad: float32 [768], P(('dp', 'fsdp'))
- span_weight_grad: float32 [768, 128], P(('dp', 'fsdp'))
- answer_vector_grad: float32 [128], P(('dp', 'fsdp'))
Inputs may be any that keep to these rules, and one draw needn't show every extreme that they name: `doc_lengths`: the 4 lengths of a pack sum to 512, and in every pack one of them is 288. `query_ids`: every query has one segment or more.
All inputs are finite; a program needn't handle non-finite values.
Results may differ from a plain program's by a relative error of at most 0.014.
Values may be sent and summed in bfloat16 or wider, within the bound.
No kernel may reach another device: no remote copies, remote signals or barrier semaphores. Data moves between devices by JAX's collectives and lax.ppermute only.
A program may use at most 192 MiB of HBM per device.

v0:
```python
import math

import jax
import jax.numpy as jnp
from jax import lax
from jax.sharding import PartitionSpec as P

HEADS = 12
HEAD_DIM = 64
PACK = 512
SEGS_PACK = 4


HIGHEST = lax.Precision.HIGHEST
MASKED = -1e30


def matmul(operand, matrix):
    return jnp.dot(operand, matrix, preferred_element_type=jnp.float32)


def weight_grad(operand, matrix):
    return lax.dot_general(
        operand, matrix, (((0,), (0,)), ((), ())), preferred_element_type=jnp.float32
    )


def back_prod(operand, matrix):
    return lax.dot_general(
        operand, matrix, (((1,), (1,)), ((), ())), preferred_element_type=jnp.float32
    )


def normalize(hidden):
    center = hidden - jnp.mean(hidden, axis=-1, keepdims=True)
    factor = lax.rsqrt(jnp.mean(center * center, axis=-1, keepdims=True) + 1e-06)
    return (center * factor, factor)


def norm_back(gradient, normed, factor):
    return factor * (
        gradient
        - jnp.mean(gradient, axis=-1, keepdims=True)
        - normed * jnp.mean(gradient * normed, axis=-1, keepdims=True)
    )


def segment_ids(lengths):
    bounds = jnp.cumsum(lengths, axis=1)
    places = lax.broadcasted_iota(jnp.int32, (1, PACK, 1), 1)
    return jnp.sum((places >= bounds[:, None, :]).astype(jnp.int32), axis=-1)


def exact_gelu(inner_pre):
    return jax.nn.gelu(inner_pre, approximate=False)


def masked_scores(query_heads, key_heads, segment):
    scaling = 1.0 / math.sqrt(query_heads.shape[-1])
    same_segment = segment[:, None] == segment[None, :]
    raw_scores = (
        jnp.einsum("qhd,khd->hqk", query_heads, key_heads, preferred_element_type=jnp.float32)
        * scaling
    )
    return jnp.where(same_segment[None], raw_scores, MASKED)


def attend(pieces):
    query_heads, key_heads, value_heads, segment = pieces
    scores = masked_scores(query_heads, key_heads, segment)
    highest = jnp.max(scores, axis=-1, keepdims=True)
    weights = jnp.exp(scores - highest)
    totals = jnp.sum(weights, axis=-1, keepdims=True)
    shares = (weights / totals).astype(jnp.bfloat16)
    context = jnp.einsum("hqk,khd->qhd", shares, value_heads, preferred_element_type=jnp.float32)
    return (context.astype(jnp.bfloat16), highest + jnp.log(totals))


def attend_back(pieces):
    query_heads, key_heads, value_heads, segment, logsum, context_grad = pieces
    scaling = 1.0 / math.sqrt(query_heads.shape[-1])
    scores = masked_scores(query_heads, key_heads, segment)
    softmax = jnp.exp(scores - logsum)
    value_grad = jnp.einsum(
        "hqk,qhd->khd",
        softmax.astype(jnp.bfloat16),
        context_grad,
        preferred_element_type=jnp.float32,
    )
    shares_grad = jnp.einsum(
        "qhd,khd->hqk", context_grad, value_heads, preferred_element_type=jnp.float32
    )
    score_grad = softmax * (shares_grad - jnp.sum(softmax * shares_grad, axis=-1, keepdims=True))
    score_low = score_grad.astype(jnp.bfloat16)
    query_grad = (
        jnp.einsum("hqk,khd->qhd", score_low, key_heads, preferred_element_type=jnp.float32)
        * scaling
    )
    key_grad = (
        jnp.einsum("hqk,qhd->khd", score_low, query_heads, preferred_element_type=jnp.float32)
        * scaling
    )
    stacked = jnp.stack([query_grad, key_grad, value_grad], axis=1)
    return stacked.reshape(stacked.shape[0], -1)


def shards(
    tokens,
    cotangent,
    doc_lengths,
    query_ids,
    qkv_weight,
    query_bias,
    value_bias,
    attn_weight,
    attn_bias,
    first_gain,
    first_shift,
    inner_weight,
    inner_bias,
    outer_weight,
    outer_bias,
    second_gain,
    second_shift,
    span_weight,
    answer_vector,
):
    rows_here = tokens.shape[0]
    width = tokens.shape[1]
    packs_here = rows_here // PACK
    gathered = (
        lax.all_gather(qkv_weight, ("dp", "fsdp"), axis=0, tiled=True),
        lax.all_gather(query_bias, ("dp", "fsdp"), axis=0, tiled=True),
        lax.all_gather(value_bias, ("dp", "fsdp"), axis=0, tiled=True),
        lax.all_gather(attn_weight, ("dp", "fsdp"), axis=0, tiled=True),
        lax.all_gather(attn_bias, ("dp", "fsdp"), axis=0, tiled=True),
        lax.all_gather(first_gain, ("dp", "fsdp"), axis=0, tiled=True),
        lax.all_gather(first_shift, ("dp", "fsdp"), axis=0, tiled=True),
        lax.all_gather(inner_weight, ("dp", "fsdp"), axis=0, tiled=True),
        lax.all_gather(inner_bias, ("dp", "fsdp"), axis=0, tiled=True),
        lax.all_gather(outer_weight, ("dp", "fsdp"), axis=0, tiled=True),
        lax.all_gather(outer_bias, ("dp", "fsdp"), axis=0, tiled=True),
        lax.all_gather(second_gain, ("dp", "fsdp"), axis=0, tiled=True),
        lax.all_gather(second_shift, ("dp", "fsdp"), axis=0, tiled=True),
        lax.all_gather(span_weight, ("dp", "fsdp"), axis=0, tiled=True),
        lax.all_gather(answer_vector, ("dp", "fsdp"), axis=0, tiled=True),
    )
    (
        mix_full,
        query_add,
        value_add,
        attn_full,
        attn_add,
        gain_one,
        shift_one,
        inner_full,
        inner_add,
        outer_full,
        outer_add,
        gain_two,
        shift_two,
        span_full,
        answer_full,
    ) = gathered
    segment = segment_ids(doc_lengths)
    qkv_add = jnp.concatenate([query_add, jnp.zeros_like(query_add), value_add]).astype(jnp.float32)
    mixed_rows = (matmul(tokens, mix_full) + qkv_add).astype(jnp.bfloat16)
    head_split = mixed_rows.reshape(packs_here, PACK, 3, HEADS, HEAD_DIM)
    query_heads = head_split[:, :, 0]
    key_heads = head_split[:, :, 1]
    value_heads = head_split[:, :, 2]
    context, logsum = lax.map(attend, (query_heads, key_heads, value_heads, segment))
    context = context.reshape(rows_here, width)
    attended = matmul(context, attn_full) + attn_add.astype(jnp.float32)
    normed_one, factor_one = normalize(tokens.astype(jnp.float32) + attended)
    first_norm = normed_one * gain_one.astype(jnp.float32) + shift_one.astype(jnp.float32)
    first_low = first_norm.astype(jnp.bfloat16)
    inner_pre = matmul(first_low, inner_full) + inner_add.astype(jnp.float32)
    active, gelu_back = jax.vjp(exact_gelu, inner_pre)
    active_low = active.astype(jnp.bfloat16)
    outer_out = matmul(active_low, outer_full) + outer_add.astype(jnp.float32)
    normed_two, factor_two = normalize(first_norm + outer_out)
    result = (normed_two * gain_two.astype(jnp.float32) + shift_two.astype(jnp.float32)).astype(
        jnp.bfloat16
    )
    span_rows = matmul(result, span_full)
    answer_wide = answer_full.astype(jnp.float32)
    token_score = jnp.dot(span_rows, answer_wide, precision=HIGHEST).reshape(packs_here, PACK)
    member = segment[:, None, :] == lax.broadcasted_iota(jnp.int32, (1, SEGS_PACK, 1), 1)
    doc_score = jax.nn.logsumexp(jnp.where(member, token_score[:, None, :], MASKED), axis=-1)
    doc_flat = doc_score.reshape(-1)
    queries_all = packs_here * lax.axis_size("dp") * lax.axis_size("fsdp")
    member_query = query_ids == lax.broadcasted_iota(jnp.int32, (1, queries_all), 1)
    local_peak = jnp.max(jnp.where(member_query, doc_flat[:, None], MASKED), axis=0)
    local_mass = jnp.sum(
        jnp.where(member_query, jnp.exp(doc_flat[:, None] - local_peak[None, :]), 0.0), axis=0
    )
    peak_score = lax.pmax(local_peak, ("dp", "fsdp"))
    mass_total = lax.psum(local_mass * jnp.exp(local_peak - peak_score), ("dp", "fsdp"))
    marginal = peak_score + jnp.log(mass_total)
    likelihood = jnp.sum(marginal)
    gathered = (
        lax.all_gather(qkv_weight, ("dp", "fsdp"), axis=0, tiled=True),
        lax.all_gather(query_bias, ("dp", "fsdp"), axis=0, tiled=True),
        lax.all_gather(value_bias, ("dp", "fsdp"), axis=0, tiled=True),
        lax.all_gather(attn_weight, ("dp", "fsdp"), axis=0, tiled=True),
        lax.all_gather(attn_bias, ("dp", "fsdp"), axis=0, tiled=True),
        lax.all_gather(first_gain, ("dp", "fsdp"), axis=0, tiled=True),
        lax.all_gather(first_shift, ("dp", "fsdp"), axis=0, tiled=True),
        lax.all_gather(inner_weight, ("dp", "fsdp"), axis=0, tiled=True),
        lax.all_gather(inner_bias, ("dp", "fsdp"), axis=0, tiled=True),
        lax.all_gather(outer_weight, ("dp", "fsdp"), axis=0, tiled=True),
        lax.all_gather(outer_bias, ("dp", "fsdp"), axis=0, tiled=True),
        lax.all_gather(second_gain, ("dp", "fsdp"), axis=0, tiled=True),
        lax.all_gather(second_shift, ("dp", "fsdp"), axis=0, tiled=True),
        lax.all_gather(span_weight, ("dp", "fsdp"), axis=0, tiled=True),
        lax.all_gather(answer_vector, ("dp", "fsdp"), axis=0, tiled=True),
    )
    (
        mix_full,
        query_add,
        value_add,
        attn_full,
        attn_add,
        gain_one,
        shift_one,
        inner_full,
        inner_add,
        outer_full,
        outer_add,
        gain_two,
        shift_two,
        span_full,
        answer_full,
    ) = gathered
    seg_marginal = jnp.sum(jnp.where(member_query, marginal[None, :], 0.0), axis=1).reshape(
        packs_here, SEGS_PACK
    )
    doc_weight = jnp.exp(doc_score - seg_marginal)
    token_weight = jnp.sum(
        jnp.where(
            member,
            doc_weight[:, :, None] * jnp.exp(token_score[:, None, :] - doc_score[:, :, None]),
            0.0,
        ),
        axis=1,
    ).reshape(rows_here)
    answer_grad = jnp.dot(token_weight, span_rows, precision=HIGHEST)
    span_grad = (token_weight[:, None] * answer_full.astype(jnp.float32)[None, :]).astype(
        jnp.bfloat16
    )
    span_weight_grad = weight_grad(result, span_grad)
    result_grad = cotangent.astype(jnp.float32) + back_prod(span_grad, span_full)
    second_gain_grad = jnp.sum(result_grad * normed_two, axis=0)
    second_shift_grad = jnp.sum(result_grad, axis=0)
    second_sum_grad = norm_back(result_grad * gain_two.astype(jnp.float32), normed_two, factor_two)
    outer_low = second_sum_grad.astype(jnp.bfloat16)
    outer_weight_grad = weight_grad(active_low, outer_low)
    outer_bias_grad = jnp.sum(outer_low.astype(jnp.float32), axis=0)
    (inner_grad,) = gelu_back(back_prod(outer_low, outer_full))
    inner_low = inner_grad.astype(jnp.bfloat16)
    inner_weight_grad = weight_grad(first_low, inner_low)
    inner_bias_grad = jnp.sum(inner_low.astype(jnp.float32), axis=0)
    first_grad = second_sum_grad + back_prod(inner_low, inner_full)
    first_gain_grad = jnp.sum(first_grad * normed_one, axis=0)
    first_shift_grad = jnp.sum(first_grad, axis=0)
    first_sum_grad = norm_back(first_grad * gain_one.astype(jnp.float32), normed_one, factor_one)
    attended_low = first_sum_grad.astype(jnp.bfloat16)
    attn_weight_grad = weight_grad(context, attended_low)
    attn_bias_grad = jnp.sum(attended_low.astype(jnp.float32), axis=0)
    context_grad = back_prod(attended_low, attn_full).astype(jnp.bfloat16)
    context_grad = context_grad.reshape(packs_here, PACK, HEADS, HEAD_DIM)
    mixed_grad = lax.map(
        attend_back, (query_heads, key_heads, value_heads, segment, logsum, context_grad)
    )
    mixed_low = mixed_grad.reshape(rows_here, 3 * width).astype(jnp.bfloat16)
    qkv_weight_grad = weight_grad(tokens, mixed_low)
    bias_sums = jnp.sum(mixed_low.astype(jnp.float32), axis=0)
    query_bias_grad = bias_sums[:width]
    value_bias_grad = bias_sums[2 * width :]
    input_grad = back_prod(mixed_low, mix_full) + first_sum_grad
    owned_grads = (
        lax.psum_scatter(qkv_weight_grad, ("dp", "fsdp"), scatter_dimension=0, tiled=True),
        lax.psum_scatter(query_bias_grad, ("dp", "fsdp"), scatter_dimension=0, tiled=True),
        lax.psum_scatter(value_bias_grad, ("dp", "fsdp"), scatter_dimension=0, tiled=True),
        lax.psum_scatter(attn_weight_grad, ("dp", "fsdp"), scatter_dimension=0, tiled=True),
        lax.psum_scatter(attn_bias_grad, ("dp", "fsdp"), scatter_dimension=0, tiled=True),
        lax.psum_scatter(first_gain_grad, ("dp", "fsdp"), scatter_dimension=0, tiled=True),
        lax.psum_scatter(first_shift_grad, ("dp", "fsdp"), scatter_dimension=0, tiled=True),
        lax.psum_scatter(inner_weight_grad, ("dp", "fsdp"), scatter_dimension=0, tiled=True),
        lax.psum_scatter(inner_bias_grad, ("dp", "fsdp"), scatter_dimension=0, tiled=True),
        lax.psum_scatter(outer_weight_grad, ("dp", "fsdp"), scatter_dimension=0, tiled=True),
        lax.psum_scatter(outer_bias_grad, ("dp", "fsdp"), scatter_dimension=0, tiled=True),
        lax.psum_scatter(second_gain_grad, ("dp", "fsdp"), scatter_dimension=0, tiled=True),
        lax.psum_scatter(second_shift_grad, ("dp", "fsdp"), scatter_dimension=0, tiled=True),
        lax.psum_scatter(span_weight_grad, ("dp", "fsdp"), scatter_dimension=0, tiled=True),
        lax.psum_scatter(answer_grad, ("dp", "fsdp"), scatter_dimension=0, tiled=True),
    )
    return (likelihood, result, input_grad) + tuple(owned_grads)


def solution(mesh):
    in_specs = (
        P(("dp", "fsdp"), None),
        P(("dp", "fsdp"), None),
        P(("dp", "fsdp"), None),
        P(("dp", "fsdp"), None),
        P(("dp", "fsdp"), None),
        P(("dp", "fsdp")),
        P(("dp", "fsdp")),
        P(("dp", "fsdp"), None),
        P(("dp", "fsdp")),
        P(("dp", "fsdp")),
        P(("dp", "fsdp")),
        P(("dp", "fsdp"), None),
        P(("dp", "fsdp")),
        P(("dp", "fsdp"), None),
        P(("dp", "fsdp")),
        P(("dp", "fsdp")),
        P(("dp", "fsdp")),
        P(("dp", "fsdp"), None),
        P(("dp", "fsdp")),
    )
    out_specs = (
        P(),
        P(("dp", "fsdp"), None),
        P(("dp", "fsdp"), None),
        P(("dp", "fsdp"), None),
        P(("dp", "fsdp")),
        P(("dp", "fsdp")),
        P(("dp", "fsdp"), None),
        P(("dp", "fsdp")),
        P(("dp", "fsdp")),
        P(("dp", "fsdp")),
        P(("dp", "fsdp"), None),
        P(("dp", "fsdp")),
        P(("dp", "fsdp"), None),
        P(("dp", "fsdp")),
        P(("dp", "fsdp")),
        P(("dp", "fsdp")),
        P(("dp", "fsdp"), None),
        P(("dp", "fsdp")),
    )
    return jax.shard_map(shards, mesh=mesh, in_specs=in_specs, out_specs=out_specs, check_vma=False)
```

profile of v0, /device:TPU:0, one launch (start us, length us, event | category | flops | bytes accessed | tf_op | source)
XLA Modules:
  0.0 978.5 jit_solution(9499859527295209149)
XLA Ops:
  19.5 42.6 %all-reduce.22 = (bf16[768]{0:T(1024)(128)(2,1)S(1)}, bf16[768]{0:T(1024)(128)(2,1)S(1)}, bf16[768]{0:T(1024)(128)(2,1)S(1)}, bf16[768]{0:T(1024)(128)(2,1)S(1)}...) all-reduce(bf16[768]{0:T(1024)(128)(2,1)S(1)} %dynamic-update-slice, ...), channel_id=1, replica_groups=mesh['dp'=8,'fsdp'=4] {'dp','fsdp'}, use_global_device_ids=true, to_apply=%add.1 | all-reduce | flops 9344 | bytes 37376
  66.5 72.8 %all_gather.66 = bf16[768,128]{1,0:T(8,128)(2,1)} all-gather(bf16[24,128]{1,0:T(8,128)(2,1)S(1)} %copy-done.34), channel_id=1, replica_groups=mesh['dp'=8,'fsdp'=4] {'dp','fsdp'}, dimensions={0}, use_global_device_ids=true | all-gather | bytes 202752 | tf_op jit(solution)/shard_map/all_gather | solution.py:145
  141.4 7.5 add_convert_fusion.1
  148.9 6.6 copy.107
  155.5 8.9 reshape.253
  164.4 5.4 slice_bitcast_fusion
  171.9 21.0 %while.22 = (s32[]{:T(128)}, bf16[2,512,12,64]{1,3,2,0:T(8,128)(2,1)}, f32[2,12,512,1]{2,1,3,0:T(8,128)S(1)}, bf16[2,512,12,64]{1,3,2,0:T(8,128)(2,1)}, s32[2,51...) while((s32[]{:T(128)}, ...), condition=%wide.region_5.6_spmd, body=%wide.region_2.5_spmd.sunk | while | flops 843704320 | bytes 42172508 | solution.py:172
  176.8 5.5 fusion.126
  187.2 5.5 fusion.126
  204.7 37.9 %multiply_convert_fusion.1 = (bf16[1024,3072]{1,0:T(8,128)(2,1)}, f32[1024,3072]{1,0:T(8,128)}, f32[1024,3072]{1,0:T(8,128)}) fusion(f32[3072]{0:T(1024)S(1)} %convert_element_type.113, bf16[768,3072]{1,0:T(8,128)(2,1)} %all-gather.9.cloned.1.call-done, f32[1024,768]{0,1:T(8,128)} %copy-done.9, f32[768]{0:T(1024)S(1)} %convert_element_type.111, ...), kind=kOutput, calls=%fused_computation.64 | convolution fusion | flops 5043388416 | bytes 39348224 | tf_op jit(solution)/shard_map/dot_general | solution.py:19
  242.6 17.6 %all-gather.11.cloned.1.call-done = bf16[3072,768]{1,0:T(8,128)(2,1)} async-done(((bf16[96,768]{1,0:T(8,128)(2,1)}), bf16[3072,768]{1,0:T(8,128)(2,1)}) %all-gather.11.cloned.1.call-update) | async-done | bytes 4718608 | tf_op jit(solution)/shard_map/all_gather | solution.py:141
  260.2 9.9 %fusion.80 = (f32[1024]{0:T(1024)S(1)}, f32[1024,768]{0,1:T(8,128)S(1)}) fusion(f32[768]{0:T(1024)S(1)} %copy-done.41, bf16[1024,3072]{1,0:T(8,128)(2,1)} %get-tuple-element.292, bf16[3072,768]{1,0:T(8,128)(2,1)} %all-gather.11.cloned.1.call-done, f32[768]{0:T(1024)S(1)} %convert_element_type.111, f32[768]{0:T(1024)S(1)} %convert_element_type.110, ...), kind=kOutput, calls=%fused_computation.156 | convolution fusion | flops 4837342208 | bytes 17323008 | tf_op jit(solution)/shard_map/dot_general | solution.py:19
  276.0 39.6 %pmax.7 = f32[64]{0:T(128)S(1)} all-reduce(f32[64]{0:T(128)S(1)} %select_reduce_fusion.4), channel_id=1, replica_groups=mesh['dp'=8,'fsdp'=4] {'dp','fsdp'}, use_global_device_ids=true, to_apply=%region_13.14 | all-reduce | flops 64 | bytes 512 | tf_op jit(solution)/shard_map/pmax | solution.py:198
  315.7 39.5 %psum.7 = f32[64]{0:T(128)S(1)} all-reduce(f32[64]{0:T(128)S(1)} %exponential_multiply_fusion), channel_id=1, replica_groups=mesh['dp'=8,'fsdp'=4] {'dp','fsdp'}, use_global_device_ids=true, to_apply=%region_15.16 | all-reduce | flops 64 | bytes 512 | tf_op jit(solution)/shard_map/psum | solution.py:199
  364.2 5.2 convert_reduce_fusion.2
  369.4 19.9 %convert_reduce_fusion = (f32[3072]{0:T(1024)}, bf16[1024,3072]{1,0:T(8,128)(2,1)}) fusion(f32[1024,3072]{1,0:T(8,128)} %get-tuple-element.293, bf16[3072,768]{1,0:T(8,128)(2,1)} %all-gather.11.cloned.1.call-done, f32[1024,768]{0,1:T(8,128)} %get-tuple-element.285, f32[1024,3072]{1,0:T(8,128)} %get-tuple-element.305, f32[3072]{0:T(1024)S(1)} %convert_element_type.113), kind=kOutput, calls=%fused_computation.62 | convolution fusion | flops 4886098944 | bytes 39346176 | tf_op jit(solution)/shard_map/dot_general | solution.py:29
  389.3 10.8 %multiply_reduce_fusion.2 = (f32[768]{0:T(1024)}, f32[1024]{0:T(1024)S(1)}, f32[1024]{0:T(1024)S(1)}, f32[768]{0:T(1024)}, f32[1024,768]{0,1:T(8,128)S(1)}) fusion(f32[1024,768]{0,1:T(8,128)S(1)} %copy-done.10, f32[1024]{0:T(1024)S(1)} %add_rsqrt_fusion.1, f32[1024]{0:T(1024)S(1)} %broadcast_multiply_fusion.5, f32[768]{0:T(1024)S(1)} %convert_element_type.110, ...), kind=kOutput, calls=%fused_computation.83 | convolution fusion | flops 4839698432 | bytes 20472832 | tf_op jit(solution)/shard_map/dot_general | solution.py:29
  408.6 5.4 fusion.64
  414.1 57.5 %while.23 = (s32[]{:T(128)}, bf16[2,512,2304]{2,1,0:T(8,128)(2,1)}, bf16[2,512,12,64]{1,3,2,0:T(8,128)(2,1)S(1)}, s32[2,512]{1,0:T(2,128)S(1)}, bf16[2,512,12,64...) while((s32[]{:T(128)}, bf16[2,512,2304]{2,1,0:T(8,128)(2,1)}, ...), condition=%wide.region_25.26_spmd, body=%wide.region_23.25_spmd.sunk | while | flops 2064640000 | bytes 149095184 | solution.py:273
  416.3 6.9 multiply_reduce_fusion.10
  423.2 7.0 multiply_convert_fusion.6
  444.8 6.9 multiply_reduce_fusion.10
  451.7 7.0 multiply_convert_fusion.6
  471.6 9.7 convolution_bitcast_fusion
  481.3 8.1 copy.134
  491.3 10.2 %fusion.67 = f32[3072,768]{1,0:T(8,128)} fusion(bf16[1024,3072]{1,0:T(8,128)(2,1)} %get-tuple-element.292, f32[1024,768]{0,1:T(8,128)S(1)} %copy-done.15), kind=kOutput, calls=%fused_computation.147 | convolution fusion | flops 4832624640 | bytes 18874368 | tf_op jit(solution)/shard_map/dot_general | solution.py:23
  503.5 10.5 %fusion.71 = f32[768,3072]{1,0:T(8,128)} fusion(bf16[1024,3072]{1,0:T(8,128)(2,1)} %get-tuple-element.311, f32[1024,768]{0,1:T(8,128)S(1)} %copy-done.11, f32[768]{0:T(1024)S(1)} %copy-done.40, f32[768]{0:T(1024)S(1)} %copy-done.29, f32[1024]{0:T(1024)S(1)} %copy-done.31, f32[1024]{0:T(1024)S(1)} %copy-done.22), kind=kOutput, calls=%fused_computation.151 | convolution fusion | flops 4835770368 | bytes 18888704 | tf_op jit(solution)/shard_map/dot_general | solution.py:23
  520.3 41.9 %all-reduce.21 = (f32[768]{0:T(1024)S(1)}, f32[768]{0:T(1024)S(1)}, f32[768]{0:T(1024)S(1)}, f32[768]{0:T(1024)S(1)}, f32[768]{0:T(1024)S(1)}, /*index=5*/f32[30...) all-reduce(f32[768]{0:T(1024)S(1)} %get-tuple-element.302, ...), channel_id=3, replica_groups=mesh['dp'=8,'fsdp'=4] {'dp','fsdp'}, use_global_device_ids=true, to_apply=%region_28.29.clone | all-reduce | flops 9344 | bytes 74752
  566.8 8.1 convolution_add_fusion.1
  578.5 109.5 %reduce-scatter.16.cloned.1.call-done = f32[24,2304]{1,0:T(8,128)} async-done(((f32[768,2304]{1,0:T(8,128)}), f32[24,2304]{1,0:T(8,128)}) %reduce-scatter.16.cloned.1.call-update) | async-done | bytes 221200
  688.0 142.1 %reduce-scatter.14.cloned.1.call-done = f32[96,768]{1,0:T(8,128)} async-done(((f32[3072,768]{1,0:T(8,128)}), f32[96,768]{1,0:T(8,128)}) %reduce-scatter.14.cloned.1.call-update) | async-done | bytes 294928 | tf_op jit(solution)/shard_map/reduce_scatter | solution.py:292
  830.2 141.3 %reduce-scatter.12.cloned.1.call-done = f32[24,3072]{1,0:T(8,128)} async-done(((f32[768,3072]{1,0:T(8,128)}), f32[24,3072]{1,0:T(8,128)}) %reduce-scatter.12.cloned.1.call-update) | async-done | bytes 294928 | tf_op jit(solution)/shard_map/reduce_scatter | solution.py:290
  (252 shorter events, 113.1 us)
Async XLA Ops:
  7.2 59.3 %copy-start.34 = (bf16[24,128]{1,0:T(8,128)(2,1)S(1)}, bf16[24,128]{1,0:T(8,128)(2,1)}, u32[]{:S(2)}) copy-start(bf16[24,128]{1,0:T(8,128)(2,1)} %param.40) | copy-start | bytes 18436
  7.2 132.5 %copy-start.16 = (bf16[1024,768]{1,0:T(8,128)(2,1)S(1)}, bf16[1024,768]{1,0:T(8,128)(2,1)}, u32[]{:S(2)}) copy-start(bf16[1024,768]{1,0:T(8,128)(2,1)} %param.24) | copy-start | bytes 4718596
  7.2 134.2 %all-gather.5.cloned.1.call-start = ((), (), s32[]{:S(2)}) async-start(), calls=%async_computation.5 | async-start | bytes 3649536 | tf_op jit(solution)/shard_map/all_gather | solution.py:132
  7.9 133.5 %copy-start.17 = (bf16[1024,768]{1,0:T(8,128)(2,1)S(1)}, bf16[1024,768]{1,0:T(8,128)(2,1)}, u32[]{:S(2)}) copy-start(bf16[1024,768]{1,0:T(8,128)(2,1)} %param.23) | copy-start | bytes 4718596
  8.0 190.7 %all-gather.7.cloned.1.call-start = ((), (), s32[]{:S(2)}) async-start(), calls=%async_computation.6 | async-start | bytes 1216512 | tf_op jit(solution)/shard_map/all_gather | solution.py:135
  8.7 196.0 %all-gather.9.cloned.1.call-start = ((), (), s32[]{:S(2)}) async-start(), calls=%async_computation.7 | async-start | bytes 4866048 | tf_op jit(solution)/shard_map/all_gather | solution.py:139
  9.4 250.7 %all-gather.11.cloned.1.call-start = ((), (), s32[]{:S(2)}) async-start(), calls=%async_computation.8 | async-start | bytes 4866048 | tf_op jit(solution)/shard_map/all_gather | solution.py:141
  10.0 568.5 %reduce-scatter.18.cloned.1.call-start = ((), (), s32[]{:S(2)}) async-start(), calls=%async_computation.13 | async-start | bytes 405504
  62.1 86.9 %copy-start.43 = (bf16[128]{0:T(256)(128)(2,1)}, bf16[128]{0:T(256)(128)(2,1)S(1)}, u32[]{:S(2)}) copy-start(bf16[128]{0:T(256)(128)(2,1)S(1)} %get-tuple-element.283) | copy-start | bytes 772
  64.6 335.4 %copy-start.28 = (f32[768]{0:T(1024)}, f32[768]{0:T(1024)S(1)}, u32[]{:S(2)}) copy-start(f32[768]{0:T(1024)S(1)} %convert_element_type.110) | copy-start | bytes 9220
  64.7 195.5 %copy-start.39 = (f32[768]{0:T(1024)}, f32[768]{0:T(1024)S(1)}, u32[]{:S(2)}) copy-start(f32[768]{0:T(1024)S(1)} %convert_element_type.111) | copy-start | bytes 9220
  192.9 9.7 copy-start
  192.9 9.7 copy-start.3
  192.9 9.7 copy-start.19
  202.6 197.5 %copy-start.21 = (f32[1024]{0:T(1024)}, f32[1024]{0:T(1024)S(1)}, u32[]{:S(2)}) copy-start(f32[1024]{0:T(1024)S(1)} %broadcast_multiply_fusion.5) | copy-start | bytes 12292
  204.7 195.4 %copy-start.30 = (f32[1024]{0:T(1024)}, f32[1024]{0:T(1024)S(1)}, u32[]{:S(2)}) copy-start(f32[1024]{0:T(1024)S(1)} %add_rsqrt_fusion.1) | copy-start | bytes 12292
  204.7 55.5 %copy-start.41 = (f32[768]{0:T(1024)S(1)}, f32[768]{0:T(1024)}, u32[]{:S(2)}) copy-start(f32[768]{0:T(1024)} %convert_element_type.115) | copy-start | bytes 9220
  260.2 10.3 %copy-start.23 = (f32[768]{0:T(1024)S(1)}, f32[768]{0:T(1024)}, u32[]{:S(2)}) copy-start(f32[768]{0:T(1024)} %convert_element_type.116) | copy-start | bytes 9220
  260.2 10.3 %copy-start.32 = (f32[768]{0:T(1024)S(1)}, f32[768]{0:T(1024)}, u32[]{:S(2)}) copy-start(f32[768]{0:T(1024)} %convert_element_type.117) | copy-start | bytes 9220
  270.5 85.7 %copy-start.42 = (f32[128]{0:T(128)S(1)}, f32[128]{0:T(128)}, u32[]{:S(2)}) copy-start(f32[128]{0:T(128)} %convert_element_type.120) | copy-start | bytes 1540
  356.2 8.0 copy-start.24
  364.2 214.3 %reduce-scatter.10.cloned.1.call-start = ((), (), s32[]{:S(2)}) async-start(), calls=%async_computation.9 | async-start | bytes 2433024 | tf_op jit(solution)/shard_map/reduce_scatter | solution.py:286
  369.4 19.9 %copy-start.10 = (f32[1024,768]{0,1:T(8,128)S(1)}, f32[1024,768]{0,1:T(8,128)}, u32[]{:S(2)}) copy-start(f32[1024,768]{0,1:T(8,128)} %copy-done.9) | copy-start | bytes 9437188
  414.0 274.0 %reduce-scatter.16.cloned.1.call-start = ((), (), s32[]{:S(2)}) async-start(), calls=%async_computation.12 | async-start | bytes 7299072
  489.4 340.7 %reduce-scatter.14.cloned.1.call-start = ((), (), s32[]{:S(2)}) async-start(), calls=%async_computation.11 | async-start | bytes 9732096 | tf_op jit(solution)/shard_map/reduce_scatter | solution.py:292
  501.6 469.8 %reduce-scatter.12.cloned.1.call-start = ((), (), s32[]{:S(2)}) async-start(), calls=%async_computation.10 | async-start | bytes 9732096 | tf_op jit(solution)/shard_map/reduce_scatter | solution.py:290
  514.0 6.2 copy-start.26
  514.0 6.2 copy-start.27
  514.0 6.2 copy-start.33
  514.1 6.2 copy-start.35
  514.1 6.2 copy-start.36
  514.1 6.2 copy-start.37
  (29 other events, 85.3 us)
Sparse Core Ops, SparseCore 0:
  10.8 63.2 all-gather.4
  76.9 52.7 all-gather.6
  132.6 62.5 all-gather.8
  197.8 62.3 all-gather.10
  364.3 94.5 reduce-scatter.17
  465.5 98.0 reduce-scatter.9
  569.8 118.1 reduce-scatter.15
  695.5 134.6 reduce-scatter.13
  836.7 134.7 reduce-scatter.11
where the time goes:
time: 983 us; the launch traced here: 978 us
  waiting for transfers between devices  413 us (42%)
  blocking collectives  236 us (24%)
  matrix products  191 us (19%)
  local copies, waits for them, and re-layouts  84.1 us (9%)
  other arithmetic  37.7 us (4%)
  between operations  15 us (2%)
    reduce_scatter x1, waiting for transfers between devices, shards(): lax.psum_scatter(outer_weight_grad, ('dp', 'fsdp'), scatter_dimension=0,...  142 us
    reduce_scatter x1, waiting for transfers between devices, shards(): lax.psum_scatter(inner_weight_grad, ('dp', 'fsdp'), scatter_dimension=0,...  141 us
    unnamed x11, waiting for transfers between devices  112 us
    unnamed x2, blocking collectives  84.5 us
    all_gather x1, blocking collectives, shards(): lax.all_gather(span_weight, ('dp', 'fsdp'), axis=0, tiled=True)  72.8 us
    dot_general x5, matrix products, matmul(): return jnp.dot(operand, matrix, preferred_element_type=jnp.float32)  61.2 us
    dot_general x5, matrix products, back_prod(): lax.dot_general(operand, matrix, (((1,), (1,)), ((), ())), preferred_elem...  45.3 us
    unnamed x123, local copies, waits for them, and re-layouts  41 us
  transfers between devices with their start and end apart: 9, of which 4 were waited for; matrix products, arithmetic and copies ran while one was open for 29% of the time, Pallas kernels for 0%

commit v1 on v0

--- a/solution.py
+++ b/solution.py
@@ -13,6 +13,49 @@
 
 HIGHEST = lax.Precision.HIGHEST
 MASKED = -1e30
+
+
+AXES = ("dp", "fsdp")
+LANES = 128
+
+
+def pack_small(parts):
+    flat = jnp.concatenate(parts, axis=-1)
+    wide = -(-flat.shape[-1] // LANES) * LANES
+    pad = [(0, 0)] * (flat.ndim - 1) + [(0, wide - flat.shape[-1])]
+    return jnp.pad(flat, pad).reshape(flat.shape[:-1] + (wide // LANES, LANES))
+
+
+def unpack_small(packed, sizes):
+    flat = packed.reshape(packed.shape[:-2] + (-1,))
+    starts = [sum(sizes[:i]) for i in range(len(sizes))]
+    return [flat[..., a : a + n] for a, n in zip(starts, sizes)]
+
+
+def exchange_small(parts, devices):
+    packed = pack_small(parts)
+    spread = jnp.broadcast_to(packed[None], (devices,) + packed.shape)
+    full = lax.all_to_all(spread, AXES, 0, 0)
+    return [v.reshape(-1) for v in unpack_small(full, [p.shape[0] for p in parts])]
+
+
+def reduce_small(parts, devices):
+    packed = pack_small([p.reshape(devices, -1) for p in parts])
+    mine = jnp.sum(lax.all_to_all(packed, AXES, 0, 0), axis=0)
+    return unpack_small(mine, [p.shape[0] // devices for p in parts])
+
+
+def split_rows(grad, devices, width):
+    low = grad.astype(jnp.bfloat16)
+    share = low.shape[0] // devices
+    blocks = low.shape[1] // width
+    low = low.reshape(devices, share, blocks, width).transpose(0, 2, 1, 3)
+    return low.reshape(devices, blocks * share, width)
+
+
+def join_rows(grad, blocks):
+    share = grad.shape[0] // blocks
+    return jnp.concatenate([grad[i * share : (i + 1) * share] for i in range(blocks)], axis=1)
 
 
 def matmul(operand, matrix):
@@ -128,40 +171,54 @@
     rows_here = tokens.shape[0]
     width = tokens.shape[1]
     packs_here = rows_here // PACK
-    gathered = (
-        lax.all_gather(qkv_weight, ("dp", "fsdp"), axis=0, tiled=True),
-        lax.all_gather(query_bias, ("dp", "fsdp"), axis=0, tiled=True),
-        lax.all_gather(value_bias, ("dp", "fsdp"), axis=0, tiled=True),
-        lax.all_gather(attn_weight, ("dp", "fsdp"), axis=0, tiled=True),
-        lax.all_gather(attn_bias, ("dp", "fsdp"), axis=0, tiled=True),
-        lax.all_gather(first_gain, ("dp", "fsdp"), axis=0, tiled=True),
-        lax.all_gather(first_shift, ("dp", "fsdp"), axis=0, tiled=True),
-        lax.all_gather(inner_weight, ("dp", "fsdp"), axis=0, tiled=True),
-        lax.all_gather(inner_bias, ("dp", "fsdp"), axis=0, tiled=True),
-        lax.all_gather(outer_weight, ("dp", "fsdp"), axis=0, tiled=True),
-        lax.all_gather(outer_bias, ("dp", "fsdp"), axis=0, tiled=True),
-        lax.all_gather(second_gain, ("dp", "fsdp"), axis=0, tiled=True),
-        lax.all_gather(second_shift, ("dp", "fsdp"), axis=0, tiled=True),
-        lax.all_gather(span_weight, ("dp", "fsdp"), axis=0, tiled=True),
-        lax.all_gather(answer_vector, ("dp", "fsdp"), axis=0, tiled=True),
-    )
+    devices = lax.axis_size("dp") * lax.axis_size("fsdp")
+    share = qkv_weight.shape[0]
+    inner_wide = inner_weight.shape[1]
+    reps = inner_wide // width
+    segs_here = packs_here * SEGS_PACK
+    smalls = (
+        query_bias,
+        value_bias,
+        attn_bias,
+        first_gain,
+        first_shift,
+        inner_bias,
+        outer_bias,
+        second_gain,
+        second_shift,
+        answer_vector,
+    )
+    small_all = exchange_small([v.astype(jnp.float32) for v in smalls] + [query_ids[:, 0].astype(jnp.float32)], devices)
     (
-        mix_full,
         query_add,
         value_add,
-        attn_full,
         attn_add,
         gain_one,
         shift_one,
-        inner_full,
         inner_add,
-        outer_full,
         outer_add,
         gain_two,
         shift_two,
-        span_full,
         answer_full,
-    ) = gathered
+        ids_all,
+    ) = small_all
+    mix_full = lax.all_gather(qkv_weight, AXES, axis=0, tiled=True)
+    rest = jnp.concatenate(
+        [attn_weight, outer_weight]
+        + [inner_weight[:, i * width : (i + 1) * width] for i in range(reps)]
+        + [span_weight.reshape(-1, width)],
+        axis=0,
+    )
+    rest_all = lax.all_gather(rest, AXES, axis=0)
+    attn_full = rest_all[:, :share].reshape(width, width)
+    outer_full = rest_all[:, share : share * (1 + reps)].reshape(inner_wide, width)
+    inner_full = (
+        rest_all[:, share * (1 + reps) : share * (1 + 2 * reps)]
+        .reshape(devices, reps, share, width)
+        .transpose(0, 2, 1, 3)
+        .reshape(width, inner_wide)
+    )
+    span_full = rest_all[:, share * (1 + 2 * reps) :].reshape(width, -1)
     segment = segment_ids(doc_lengths)
     qkv_add = jnp.concatenate([query_add, jnp.zeros_like(query_add), value_add]).astype(jnp.float32)
     mixed_rows = (matmul(tokens, mix_full) + qkv_add).astype(jnp.bfloat16)
@@ -188,54 +245,14 @@
     token_score = jnp.dot(span_rows, answer_wide, precision=HIGHEST).reshape(packs_here, PACK)
     member = segment[:, None, :] == lax.broadcasted_iota(jnp.int32, (1, SEGS_PACK, 1), 1)
     doc_score = jax.nn.logsumexp(jnp.where(member, token_score[:, None, :], MASKED), axis=-1)
-    doc_flat = doc_score.reshape(-1)
-    queries_all = packs_here * lax.axis_size("dp") * lax.axis_size("fsdp")
-    member_query = query_ids == lax.broadcasted_iota(jnp.int32, (1, queries_all), 1)
-    local_peak = jnp.max(jnp.where(member_query, doc_flat[:, None], MASKED), axis=0)
-    local_mass = jnp.sum(
-        jnp.where(member_query, jnp.exp(doc_flat[:, None] - local_peak[None, :]), 0.0), axis=0
-    )
-    peak_score = lax.pmax(local_peak, ("dp", "fsdp"))
-    mass_total = lax.psum(local_mass * jnp.exp(local_peak - peak_score), ("dp", "fsdp"))
-    marginal = peak_score + jnp.log(mass_total)
+    (scores_all,) = exchange_small([doc_score.reshape(-1)], devices)
+    member_query = ids_all[None, :] == lax.broadcasted_iota(jnp.float32, (packs_here * devices, 1), 0)
+    marginal = jax.nn.logsumexp(jnp.where(member_query, scores_all[None, :], MASKED), axis=1)
     likelihood = jnp.sum(marginal)
-    gathered = (
-        lax.all_gather(qkv_weight, ("dp", "fsdp"), axis=0, tiled=True),
-        lax.all_gather(query_bias, ("dp", "fsdp"), axis=0, tiled=True),
-        lax.all_gather(value_bias, ("dp", "fsdp"), axis=0, tiled=True),
-        lax.all_gather(attn_weight, ("dp", "fsdp"), axis=0, tiled=True),
-        lax.all_gather(attn_bias, ("dp", "fsdp"), axis=0, tiled=True),
-        lax.all_gather(first_gain, ("dp", "fsdp"), axis=0, tiled=True),
-        lax.all_gather(first_shift, ("dp", "fsdp"), axis=0, tiled=True),
-        lax.all_gather(inner_weight, ("dp", "fsdp"), axis=0, tiled=True),
-        lax.all_gather(inner_bias, ("dp", "fsdp"), axis=0, tiled=True),
-        lax.all_gather(outer_weight, ("dp", "fsdp"), axis=0, tiled=True),
-        lax.all_gather(outer_bias, ("dp", "fsdp"), axis=0, tiled=True),
-        lax.all_gather(second_gain, ("dp", "fsdp"), axis=0, tiled=True),
-        lax.all_gather(second_shift, ("dp", "fsdp"), axis=0, tiled=True),
-        lax.all_gather(span_weight, ("dp", "fsdp"), axis=0, tiled=True),
-        lax.all_gather(answer_vector, ("dp", "fsdp"), axis=0, tiled=True),
-    )
-    (
-        mix_full,
-        query_add,
-        value_add,
-        attn_full,
-        attn_add,
-        gain_one,
-        shift_one,
-        inner_full,
-        inner_add,
-        outer_full,
-        outer_add,
-        gain_two,
-        shift_two,
-        span_full,
-        answer_full,
-    ) = gathered
-    seg_marginal = jnp.sum(jnp.where(member_query, marginal[None, :], 0.0), axis=1).reshape(
-        packs_here, SEGS_PACK
-    )
+    own_query = query_ids.astype(jnp.float32) == ids_all[None, :]
+    seg_marginal = jax.nn.logsumexp(
+        jnp.where(own_query, scores_all[None, :], MASKED), axis=1
+    ).reshape(packs_here, SEGS_PACK)
     doc_weight = jnp.exp(doc_score - seg_marginal)
     token_weight = jnp.sum(
         jnp.where(
@@ -260,6 +277,15 @@
     (inner_grad,) = gelu_back(back_prod(outer_low, outer_full))
     inner_low = inner_grad.astype(jnp.bfloat16)
     inner_weight_grad = weight_grad(first_low, inner_low)
+    early = jnp.concatenate(
+        [
+            outer_weight_grad.astype(jnp.bfloat16).reshape(devices, reps * share, width),
+            split_rows(inner_weight_grad, devices, width),
+            span_weight_grad.astype(jnp.bfloat16).reshape(devices, -1, width),
+        ],
+        axis=1,
+    )
+    early_own = lax.psum_scatter(early, AXES, scatter_dimension=0)
     inner_bias_grad = jnp.sum(inner_low.astype(jnp.float32), axis=0)
     first_grad = second_sum_grad + back_prod(inner_low, inner_full)
     first_gain_grad = jnp.sum(first_grad * normed_one, axis=0)
@@ -279,22 +305,57 @@
     query_bias_grad = bias_sums[:width]
     value_bias_grad = bias_sums[2 * width :]
     input_grad = back_prod(mixed_low, mix_full) + first_sum_grad
+    late = jnp.concatenate(
+        [
+            split_rows(qkv_weight_grad, devices, width),
+            split_rows(attn_weight_grad, devices, width),
+        ],
+        axis=1,
+    )
+    late_own = lax.psum_scatter(late, AXES, scatter_dimension=0)
+    small_grads = (
+        query_bias_grad,
+        value_bias_grad,
+        attn_bias_grad,
+        first_gain_grad,
+        first_shift_grad,
+        inner_bias_grad,
+        outer_bias_grad,
+        second_gain_grad,
+        second_shift_grad,
+        answer_grad,
+    )
+    own_small = reduce_small(small_grads, devices)
+    (
+        query_bias_own,
+        value_bias_own,
+        attn_bias_own,
+        first_gain_own,
+        first_shift_own,
+        inner_bias_own,
+        outer_bias_own,
+        second_gain_own,
+        second_shift_own,
+        answer_own,
+    ) = own_small
+    late_own = late_own.astype(jnp.float32)
+    early_own = early_own.astype(jnp.float32)
     owned_grads = (
-        lax.psum_scatter(qkv_weight_grad, ("dp", "fsdp"), scatter_dimension=0, tiled=True),
-        lax.psum_scatter(query_bias_grad, ("dp", "fsdp"), scatter_dimension=0, tiled=True),
-        lax.psum_scatter(value_bias_grad, ("dp", "fsdp"), scatter_dimension=0, tiled=True),
-        lax.psum_scatter(attn_weight_grad, ("dp", "fsdp"), scatter_dimension=0, tiled=True),
-        lax.psum_scatter(attn_bias_grad, ("dp", "fsdp"), scatter_dimension=0, tiled=True),
-        lax.psum_scatter(first_gain_grad, ("dp", "fsdp"), scatter_dimension=0, tiled=True),
-        lax.psum_scatter(first_shift_grad, ("dp", "fsdp"), scatter_dimension=0, tiled=True),
-        lax.psum_scatter(inner_weight_grad, ("dp", "fsdp"), scatter_dimension=0, tiled=True),
-        lax.psum_scatter(inner_bias_grad, ("dp", "fsdp"), scatter_dimension=0, tiled=True),
-        lax.psum_scatter(outer_weight_grad, ("dp", "fsdp"), scatter_dimension=0, tiled=True),
-        lax.psum_scatter(outer_bias_grad, ("dp", "fsdp"), scatter_dimension=0, tiled=True),
-        lax.psum_scatter(second_gain_grad, ("dp", "fsdp"), scatter_dimension=0, tiled=True),
-        lax.psum_scatter(second_shift_grad, ("dp", "fsdp"), scatter_dimension=0, tiled=True),
-        lax.psum_scatter(span_weight_grad, ("dp", "fsdp"), scatter_dimension=0, tiled=True),
-        lax.psum_scatter(answer_grad, ("dp", "fsdp"), scatter_dimension=0, tiled=True),
+        join_rows(late_own[: 3 * share], 3),
+        query_bias_own,
+        value_bias_own,
+        late_own[3 * share :],
+        attn_bias_own,
+        first_gain_own,
+        first_shift_own,
+        join_rows(early_own[reps * share : 2 * reps * share], reps),
+        inner_bias_own,
+        early_own[: reps * share],
+        outer_bias_own,
+        second_gain_own,
+        second_shift_own,
+        early_own[2 * reps * share :].reshape(share, -1),
+        answer_own,
     )
     return (likelihood, result, input_grad) + tuple(owned_grads)
 

time: 983 us -> 659 us (0.67)
  blocking collectives: 236 us -> 0 us
  waiting for transfers between devices: 413 us -> 252 us
  local copies, waits for them, and re-layouts: 84.1 us -> 130 us
  starting transfers between devices: 0.36 us -> 13.1 us
    unnamed x11 -> x4, waiting for transfers between devices: 112 us -> 0.73 us
    reduce_scatter x3 -> x2, waiting for transfers between devices: 283 us -> 173 us  [the longest x1 141 us: shards(): early_own = lax.psum_scatter(early, AXES, scatter_dimension=0)]
    unnamed x2 -> x0, blocking collectives: 84.5 us -> none
    all_gather x1 -> x0, blocking collectives: 72.8 us -> none  [shards(): lax.all_gather(span_weight, ('dp', 'fsdp'), axis=0, tiled=True)]
    all_gather x4 -> x2, waiting for transfers between devices: 17.6 us -> 64.6 us  [the longest x1 33.1 us: shards(): rest_all = lax.all_gather(rest, AXES, axis=0)]
    pmax x1 -> x0, blocking collectives: 39.6 us -> none  [shards(): peak_score = lax.pmax(local_peak, ('dp', 'fsdp'))]
    psum x1 -> x0, blocking collectives: 39.5 us -> none  [shards(): lax.psum(local_mass * jnp.exp(local_peak - peak_score), ('dp', 'fsdp'))]
    reshape x1 -> x21, local copies, waits for them, and re-layouts: 0.08 us -> 21.3 us  [the longest x2 15.2 us: split_rows(): low = low.reshape(devices, share, blocks, width).transpose(0, 2, 1, 3)]
  transfers between devices with their start and end apart: 9 -> 7, of which waited for: 4 -> 7; matrix products, arithmetic and copies ran while one was open for 29% -> 23% of each run, Pallas kernels for 0% -> 0%
where the time goes in v1:
time: 659 us; the launch traced here: 648 us
  waiting for transfers between devices  252 us (38%)
  matrix products  189 us (29%)
  local copies, waits for them, and re-layouts  130 us (20%)
  other arithmetic  47.2 us (7%)
  between operations  15.3 us (2%)
  starting transfers between devices  13.1 us (2%)
    reduce_scatter x1, waiting for transfers between devices, shards(): early_own = lax.psum_scatter(early, AXES, scatter_dimension=0)  141 us
    dot_general x5, matrix products, matmul(): return jnp.dot(operand, matrix, preferred_element_type=jnp.float32)  64.5 us
    dot_general x5, matrix products, back_prod(): lax.dot_general(operand, matrix, (((1,), (1,)), ((), ())), preferred_elem...  45.4 us
    all_gather x1, waiting for transfers between devices, shards(): rest_all = lax.all_gather(rest, AXES, axis=0)  33.1 us
    reduce_scatter x1, waiting for transfers between devices, shards(): late_own = lax.psum_scatter(late, AXES, scatter_dimension=0)  31.7 us
    all_gather x1, waiting for transfers between devices, shards(): mix_full = lax.all_gather(qkv_weight, AXES, axis=0, tiled=True)  31.4 us
    dot_general x5, matrix products, weight_grad(): lax.dot_general(operand, matrix, (((0,), (0,)), ((), ())), preferred_elem...  30.6 us
    unnamed x138, local copies, waits for them, and re-layouts  20.8 us
  transfers between devices with their start and end apart: 7, of which 7 were waited for; matrix products, arithmetic and copies ran while one was open for 23% of the time, Pallas kernels for 0%

profile of v1, /device:TPU:0, one launch (start us, length us, event | category | flops | bytes accessed | tf_op | source)
XLA Modules:
  0.0 647.9 jit_solution(5691056523751936494)
XLA Ops:
  14.9 6.8 %concatenate.24 = f32[300]{0:T(512)S(1)} concatenate(bf16[24]{0:T(256)(128)(2,1)} %param.28, bf16[24]{0:T(256)(128)(2,1)} %param.29, bf16[24]{0:T(256)(128)(2,1)} %param.31, bf16[24]{0:T(256)(128)(2,1)} %param.32, bf16[24]{0:T(256)(128)(2,1)} %param.33, bf16[96]{0:T(256)(128)(2,1)} %param.35, bf16[24]{0:T(256)(128)(2,1)} %param.37, bf16[24]{0:T(256)(128)(2,1)} %param.38, ...), dimensions={0} | concatenate | bytes 1816 | tf_op jit(solution)/shard_map/concatenate | solution.py:23
  22.3 7.3 %all-to-all-start = ((f32[32,3,128]{2,1,0:T(4,128)}), f32[32,3,128]{2,1,0:T(4,128)S(1)}, u32[]{:S(2)}, u32[]{:S(2)}) async-start(f32[32,3,128]{2,1,0:T(4,128)} %broadcast_in_dim.125), calls=%async_computation | async-start | bytes 131072 | tf_op jit(solution)/shard_map/all_to_all | solution.py:38
  43.0 31.4 %all-gather.5.cloned.1.call-done = bf16[768,2304]{1,0:T(8,128)(2,1)} async-done(((bf16[24,2304]{1,0:T(8,128)(2,1)}), bf16[768,2304]{1,0:T(8,128)(2,1)}) %all-gather.5.cloned.1.call-update) | async-done | bytes 3538960 | tf_op jit(solution)/shard_map/all_gather | solution.py:205
  74.5 7.4 %add_convert_fusion.1 = bf16[1024,2304]{1,0:T(8,128)(2,1)} fusion(bf16[1024,768]{1,0:T(8,128)(2,1)S(1)} %copy-done.18, bf16[768,2304]{1,0:T(8,128)(2,1)} %all-gather.5.cloned.1.call-done, f32[2304]{0:T(1024)S(1)} %pad_maximum_fusion.5), kind=kOutput, calls=%fused_computation.80 | convolution fusion | flops 3628597248 | bytes 9839616 | tf_op jit(solution)/shard_map/dot_general | solution.py:62
  81.9 6.7 %copy.143 = bf16[1024,2304]{0,1:T(8,128)(2,1)} copy(bf16[1024,2304]{1,0:T(8,128)(2,1)} %add_convert_fusion.1) | data formatting | bytes 9437184 | tf_op jit(solution)/shard_map/convert_element_type | solution.py:224
  88.6 8.9 %reshape.376 = bf16[2,512,3,12,64]{1,0,4,3,2:T(2,128)(2,1)} reshape(bf16[1024,2304]{0,1:T(8,128)(2,1)} %copy.143) | data formatting | bytes 9437184 | tf_op jit(solution)/shard_map/reshape | solution.py:225
  97.5 5.4 slice_bitcast_fusion
  105.0 21.0 %while.22 = (s32[]{:T(128)}, bf16[2,512,12,64]{1,3,2,0:T(8,128)(2,1)}, f32[2,12,512,1]{2,1,3,0:T(8,128)S(1)}, bf16[2,512,12,64]{1,3,2,0:T(8,128)(2,1)}, s32[2,51...) while((s32[]{:T(128)}, ...), condition=%wide.region_5.6_spmd, body=%wide.region_2.5_spmd.sunk | while | flops 843704320 | bytes 42172516 | solution.py:229
  109.8 5.5 fusion.133
  120.2 5.5 fusion.133
  131.8 33.1 %all-gather.7.cloned.1.call-done = bf16[32,220,768]{2,1,0:T(8,128)(2,1)} async-done(((bf16[1,220,768]{2,1,0:T(8,128)(2,1)}), bf16[32,220,768]{2,1,0:T(8,128)(2,1)}) %all-gather.7.cloned.1.call-update) | async-done | bytes 10813456 | tf_op jit(solution)/shard_map/all_gather | solution.py:212
  166.1 6.6 %fusion.81 = (bf16[32,96,768]{2,1,0:T(8,128)(2,1)}, bf16[32,96,768]{2,1,0:T(8,128)(2,1)S(1)}) fusion(bf16[32,220,768]{2,1,0:T(8,128)(2,1)} %all-gather.7.cloned.1.call-done), kind=kLoop, calls=%fused_computation.187 | loop fusion | bytes 18874368 | tf_op jit(solution)/shard_map/slice | solution.py:214
  180.7 48.9 %multiply_convert_fusion.1 = (bf16[1024,3072]{1,0:T(8,128)(2,1)S(1)}, f32[1024,3072]{1,0:T(8,128)}, f32[1024,3072]{1,0:T(8,128)}) fusion(f32[3072]{0:T(1024)S(1)} %copy-done.43, bf16[768,3072]{1,0:T(8,128)(2,1)S(1)} %bitcast.206, f32[1024,768]{0,1:T(8,128)S(1)} %get-tuple-element.341, f32[768]{0:T(1024)S(1)} %copy-done.49, f32[768]{0:T(1024)S(1)} %copy-done.36, ...), kind=kOutput, calls=%fused_computation.64 | convolution fusion | flops 5043388416 | bytes 39348224 | tf_op jit(solution)/shard_map/dot_general | solution.py:62
  229.7 5.8 fusion.86
  258.7 19.6 %convert_reduce_fusion = (f32[3072]{0:T(1024)}, bf16[1024,3072]{1,0:T(8,128)(2,1)}) fusion(f32[1024,3072]{1,0:T(8,128)} %get-tuple-element.304, bf16[3072,768]{1,0:T(8,128)(2,1)} %bitcast.212, f32[1024,768]{0,1:T(8,128)} %get-tuple-element.298, f32[1024,3072]{1,0:T(8,128)} %get-tuple-element.342, f32[3072]{0:T(1024)S(1)} %copy-done.43), kind=kOutput, calls=%fused_computation.62 | convolution fusion | flops 4886098944 | bytes 39346176 | tf_op jit(solution)/shard_map/dot_general | solution.py:72
  278.3 10.9 %multiply_reduce_fusion.2 = (f32[768]{0:T(1024)}, f32[1024]{0:T(1024)S(1)}, f32[1024]{0:T(1024)S(1)}, f32[768]{0:T(1024)}, f32[1024,768]{0,1:T(8,128)S(1)}) fusion(f32[1024,768]{0,1:T(8,128)S(1)} %copy-done.12, f32[1024]{0:T(1024)S(1)} %add_rsqrt_fusion.1, f32[1024]{0:T(1024)S(1)} %broadcast_multiply_fusion.5, f32[768]{0:T(1024)S(1)} %copy-done.36, ...), kind=kOutput, calls=%fused_computation.88 | convolution fusion | flops 4839698432 | bytes 20472832 | tf_op jit(solution)/shard_map/dot_general | solution.py:72
  305.6 58.7 %while.23 = (s32[]{:T(128)}, bf16[2,512,2304]{2,1,0:T(8,128)(2,1)}, bf16[2,512,12,64]{1,3,2,0:T(8,128)(2,1)S(1)}, s32[2,512]{1,0:T(2,128)S(1)}, bf16[2,512,12,64...) while((s32[]{:T(128)}, bf16[2,512,2304]{2,1,0:T(8,128)(2,1)}, ...), condition=%wide.region_24.25_spmd, body=%wide.region_22.24_spmd.sunk | while | flops 2064640000 | bytes 145948944 | solution.py:299
  311.6 6.9 %multiply_reduce_fusion.10 = (f32[12,512]{1,0:T(8,128)S(1)}, f32[12,512,512]{1,2,0:T(8,128)}) fusion(f32[12,512,512]{1,2,0:T(8,128)S(1)} %fusion.142, f32[12,512]{1,0:T(8,128)S(1)} %dynamic-slice_bitcast_fusion.2, pred[512,512]{0,1:T(8,128)(4,1)S(1)} %broadcast_compare_fusion.5, bf16[2,512,12,64]{1,3,2,0:T(8,128)(2,1)S(1)} %copy-done.7, ...), kind=kOutput, calls=%fused_computation.24.clone.1 | convolution fusion | flops 418375680 | bytes 27059200 | tf_op jit(solution)/shard_map/while/body/eval_jaxpr/qhd,khd->hqk/dot_general | solution.py:133
  318.5 7.0 %multiply_convert_fusion.6 = bf16[12,512,512]{1,2,0:T(8,128)(2,1)S(1)} fusion(f32[12,512,512]{1,2,0:T(8,128)} %get-tuple-element.449, f32[12,512,512]{1,2,0:T(8,128)S(1)} %fusion.142, f32[12,512]{1,0:T(8,128)S(1)} %get-tuple-element.450, f32[12,512]{1,0:T(8,128)S(1)} %dynamic-slice_bitcast_fusion.2, pred[512,512]{0,1:T(8,128)(4,1)S(1)} %broadcast_compare_fusion.5), kind=kLoop, calls=%fused_computation.23.clone.1 | loop fusion | flops 18874368 | bytes 31768576 | tf_op jit(solution)/shard_map/while/body/eval_jaxpr/convert_element_type | solution.py:137
  340.9 6.9 %multiply_reduce_fusion.10 = (f32[12,512]{1,0:T(8,128)S(1)}, f32[12,512,512]{1,2,0:T(8,128)}) fusion(f32[12,512,512]{1,2,0:T(8,128)S(1)} %fusion.142, f32[12,512]{1,0:T(8,128)S(1)} %dynamic-slice_bitcast_fusion.2, pred[512,512]{0,1:T(8,128)(4,1)S(1)} %broadcast_compare_fusion.5, bf16[2,512,12,64]{1,3,2,0:T(8,128)(2,1)S(1)} %copy-done.7, ...), kind=kOutput, calls=%fused_computation.24.clone.1 | convolution fusion | flops 418375680 | bytes 27059200 | tf_op jit(solution)/shard_map/while/body/eval_jaxpr/qhd,khd->hqk/dot_general | solution.py:133
  347.7 7.0 %multiply_convert_fusion.6 = bf16[12,512,512]{1,2,0:T(8,128)(2,1)S(1)} fusion(f32[12,512,512]{1,2,0:T(8,128)} %get-tuple-element.449, f32[12,512,512]{1,2,0:T(8,128)S(1)} %fusion.142, f32[12,512]{1,0:T(8,128)S(1)} %get-tuple-element.450, f32[12,512]{1,0:T(8,128)S(1)} %dynamic-slice_bitcast_fusion.2, pred[512,512]{0,1:T(8,128)(4,1)S(1)} %broadcast_compare_fusion.5), kind=kLoop, calls=%fused_computation.23.clone.1 | loop fusion | flops 18874368 | bytes 31768576 | tf_op jit(solution)/shard_map/while/body/eval_jaxpr/convert_element_type | solution.py:137
  364.2 8.5 %fusion.53 = bf16[768,2304]{0,1:T(8,128)(2,1)} fusion(bf16[1024,2304]{1,0:T(8,128)(2,1)} %bitcast.208, bf16[1024,768]{1,0:T(8,128)(2,1)} %param.23), kind=kOutput, calls=%fused_computation.85 | convolution fusion | flops 3625648128 | bytes 9830400 | tf_op jit(solution)/shard_map/dot_general | solution.py:66
  372.7 4.3 copy.160
  377.0 5.4 reshape.388
  390.6 10.2 %convolution_convert_fusion = bf16[768,3072]{1,0:T(8,128)(2,1)} fusion(bf16[1024,3072]{1,0:T(8,128)(2,1)} %get-tuple-element.348, f32[1024,768]{0,1:T(8,128)} %copy-done.11, f32[768]{0:T(1024)S(1)} %copy-done.50, f32[768]{0:T(1024)S(1)} %copy-done.37, f32[1024]{0:T(1024)S(1)} %copy-done.42, f32[1024]{0:T(1024)S(1)} %copy-done.33), kind=kOutput, calls=%fused_computation.81 | convolution fusion | flops 4838129664 | bytes 14170112 | tf_op jit(solution)/shard_map/dot_general | solution.py:66
  400.7 9.8 %reshape.402 = bf16[32,24,4,768]{3,2,1,0:T(4,128)(2,1)} reshape(bf16[768,3072]{1,0:T(8,128)(2,1)} %convolution_convert_fusion) | data formatting | bytes 9437184 | tf_op jit(solution)/shard_map/reshape | solution.py:52
  414.1 8.8 %convolution_convert_fusion.1 = bf16[3072,768]{1,0:T(8,128)(2,1)S(1)} fusion(bf16[1024,3072]{1,0:T(8,128)(2,1)} %copy-done.64, f32[1024,768]{0,1:T(8,128)S(1)} %copy-done.17), kind=kOutput, calls=%fused_computation.82 | convolution fusion | flops 4834983936 | bytes 14155776 | tf_op jit(solution)/shard_map/dot_general | solution.py:66
  422.8 7.8 %pad_maximum_fusion.1 = bf16[32,196,768]{2,1,0:T(8,128)(2,1)} fusion(bf16[32,4,768]{2,1,0:T(4,128)(2,1)S(1)} %reshape.404, bf16[32,96,768]{2,1,0:T(8,128)(2,1)S(1)} %bitcast.201, bf16[32,96,768]{2,1,0:T(8,128)(2,1)S(1)} %bitcast.216), kind=kLoop, calls=%fused_computation.78 | loop fusion | flops 28901376 | bytes 19267584 | tf_op jit(solution)/shard_map/concatenate | solution.py:280
  434.7 8.7 %convolution_add_fusion.1 = f32[1024,768]{0,1:T(8,128)S(1)} fusion(f32[1024,768]{0,1:T(8,128)} %copy-done.16, bf16[1024,2304]{1,0:T(8,128)(2,1)} %bitcast.209, bf16[768,2304]{1,0:T(8,128)(2,1)} %all-gather.5.cloned.1.call-done), kind=kOutput, calls=%fused_computation.107 | convolution fusion | flops 3624665088 | bytes 14548992 | tf_op jit(solution)/shard_map/dot_general | solution.py:72
  453.4 6.5 %all-to-all-done.2 = f32[32,3,128]{2,1,0:T(4,128)S(1)} async-done(((f32[32,3,128]{2,1,0:T(4,128)}), f32[32,3,128]{2,1,0:T(4,128)S(1)}, u32[]{:S(2)}, u32[]{:S(2)}) %all-to-all-start.2) | async-done | bytes 49184 | tf_op jit(solution)/shard_map/all_to_all | solution.py:44
  461.7 31.7 %reduce-scatter.3.cloned.1.call-done = bf16[1,96,768]{2,1,0:T(8,128)(2,1)} async-done(((bf16[32,96,768]{2,1,0:T(8,128)(2,1)}), bf16[1,96,768]{2,1,0:T(8,128)(2,1)}) %reduce-scatter.3.cloned.1.call-update) | async-done | bytes 147472 | tf_op jit(solution)/shard_map/reduce_scatter | solution.py:315
  495.7 141.4 %reduce-scatter.5.cloned.1.call-done = bf16[1,196,768]{2,1,0:T(8,128)(2,1)} async-done(((bf16[32,196,768]{2,1,0:T(8,128)(2,1)}), bf16[1,196,768]{2,1,0:T(8,128)(2,1)}) %reduce-scatter.5.cloned.1.call-update) | async-done | bytes 301072 | tf_op jit(solution)/shard_map/reduce_scatter | solution.py:288
  (318 shorter events, 151.4 us)
Async XLA Ops:
  7.2 67.3 %copy-start.18 = (bf16[1024,768]{1,0:T(8,128)(2,1)S(1)}, bf16[1024,768]{1,0:T(8,128)(2,1)}, u32[]{:S(2)}) copy-start(bf16[1024,768]{1,0:T(8,128)(2,1)} %param.23) | copy-start | bytes 4718596
  7.2 67.3 %all-gather.5.cloned.1.call-start = ((), (), s32[]{:S(2)}) async-start(), calls=%async_computation.5 | async-start | bytes 3649536 | tf_op jit(solution)/shard_map/all_gather | solution.py:205
  7.9 157.1 %all-gather.7.cloned.1.call-start = ((), (), s32[]{:S(2)}) async-start(), calls=%async_computation.8 | async-start | bytes 11354112 | tf_op jit(solution)/shard_map/all_gather | solution.py:212
  14.9 22.3 %copy-start.60 = (f32[8]{0:T(128)}, f32[8]{0:T(128)S(1)}, u32[]{:S(2)}) copy-start(f32[8]{0:T(128)S(1)} %convert_bitcast_fusion) | copy-start | bytes 100
  22.3 14.9 %all-to-all-start = ((f32[32,3,128]{2,1,0:T(4,128)}), f32[32,3,128]{2,1,0:T(4,128)S(1)}, u32[]{:S(2)}, u32[]{:S(2)}) async-start(f32[32,3,128]{2,1,0:T(4,128)} %broadcast_in_dim.125), calls=%async_computation | async-start | bytes 131072 | tf_op jit(solution)/shard_map/all_to_all | solution.py:38
  37.2 44.6 %copy-start.25 = (f32[4,8,3,128]{3,1,2,0:T(8,128)}, f32[4,8,3,128]{3,1,2,0:T(8,128)S(1)}, u32[]{:S(2)}) copy-start(f32[4,8,3,128]{3,1,2,0:T(8,128)S(1)} %copy.212) | copy-start | bytes 147460
  37.3 44.6 %copy-start.29 = (f32[32,4]{1,0:T(8,128)}, f32[32,4]{1,0:T(8,128)S(1)}, u32[]{:S(2)}) copy-start(f32[32,4]{1,0:T(8,128)S(1)} %slice.259) | copy-start | bytes 1540
  126.0 46.7 %copy-start = (bf16[2,512,12,64]{1,3,2,0:T(8,128)(2,1)}, bf16[2,512,12,64]{1,3,2,0:T(8,128)(2,1)S(1)}, u32[]{:S(2)}) copy-start(bf16[2,512,12,64]{1,3,2,0:T(8,128)(2,1)S(1)} %get-tuple-element.506) | copy-start | bytes 4718596
  126.0 46.7 %copy-start.3 = (bf16[2,512,12,64]{1,3,2,0:T(8,128)(2,1)}, bf16[2,512,12,64]{1,3,2,0:T(8,128)(2,1)S(1)}, u32[]{:S(2)}) copy-start(bf16[2,512,12,64]{1,3,2,0:T(8,128)(2,1)S(1)} %get-tuple-element.517) | copy-start | bytes 4718596
  178.5 51.2 %slice-start = ((s8[4718592]{0:T(1024)(128)(4,1)}), s8[4194304]{0:T(1024)(128)(4,1)S(1)}, s32[]{:S(2)}) async-start(s8[4718592]{0:T(1024)(128)(4,1)} %bitcast.213), calls=%async_computation.9 | async-start | bytes 8388608
  180.2 49.4 %copy-start.11 = (f32[1024,768]{0,1:T(8,128)}, f32[1024,768]{0,1:T(8,128)S(1)}, u32[]{:S(2)}) copy-start(f32[1024,768]{0,1:T(8,128)S(1)} %get-tuple-element.341) | copy-start | bytes 9437188
  180.2 108.9 %copy-start.32 = (f32[1024]{0:T(1024)}, f32[1024]{0:T(1024)S(1)}, u32[]{:S(2)}) copy-start(f32[1024]{0:T(1024)S(1)} %broadcast_multiply_fusion.5) | copy-start | bytes 12292
  180.6 108.5 %copy-start.41 = (f32[1024]{0:T(1024)}, f32[1024]{0:T(1024)S(1)}, u32[]{:S(2)}) copy-start(f32[1024]{0:T(1024)S(1)} %add_rsqrt_fusion.1) | copy-start | bytes 12292
  180.7 49.0 %slice-start.1 = ((s8[4718592]{0:T(1024)(128)(4,1)}), s8[524288]{0:T(1024)(128)(4,1)S(1)}, s32[]{:S(2)}) async-start(s8[4718592]{0:T(1024)(128)(4,1)} %bitcast.213), calls=%async_computation.10 | async-start | bytes 1048576
  180.7 49.0 %copy-start.55 = (f32[768]{0:T(1024)S(1)}, f32[768]{0:T(1024)}, u32[]{:S(2)}) copy-start(f32[768]{0:T(1024)} %add.157) | copy-start | bytes 9220
  229.7 6.3 copy-start.31
  229.7 6.3 copy-start.40
  236.0 10.5 %copy-start.30 = (f32[32,4]{1,0:T(8,128)S(1)}, f32[32,4]{1,0:T(8,128)}, u32[]{:S(2)}) copy-start(f32[32,4]{1,0:T(8,128)} %copy-done.29) | copy-start | bytes 1540
  236.0 15.0 %copy-start.61 = (f32[8]{0:T(128)S(1)}, f32[8]{0:T(128)}, u32[]{:S(2)}) copy-start(f32[8]{0:T(128)} %copy-done.60) | copy-start | bytes 100
  240.8 10.1 %all-to-all-start.1 = ((f32[32,1,128]{2,1,0:T(1,128)}), f32[32,1,128]{2,1,0:T(1,128)S(1)}, u32[]{:S(2)}, u32[]{:S(2)}) async-start(f32[32,1,128]{2,1,0:T(1,128)} %broadcast_in_dim.131), calls=%async_computation.1 | async-start | bytes 32768 | tf_op jit(solution)/shard_map/all_to_all | solution.py:38
  243.9 249.5 %reduce-scatter.3.cloned.1.call-start = ((), (), s32[]{:S(2)}) async-start(), calls=%async_computation.6 | async-start | bytes 4866048 | tf_op jit(solution)/shard_map/reduce_scatter | solution.py:315
  246.7 12.1 %copy-start.62 = (f32[128]{0:T(128)}, f32[128]{0:T(128)S(1)}, u32[]{:S(2)}) copy-start(f32[128]{0:T(128)S(1)} %reshape.385) | copy-start | bytes 1540
  247.6 11.2 %copy-start.45 = (f32[256]{0:T(256)}, f32[256]{0:T(256)S(1)}, u32[]{:S(2)}) copy-start(f32[256]{0:T(256)S(1)} %eq.79) | copy-start | bytes 3076
  251.8 6.9 %copy-start.34 = (f32[2,512]{1,0:T(2,128)}, f32[2,512]{1,0:T(2,128)S(1)}, u32[]{:S(2)}) copy-start(f32[2,512]{1,0:T(2,128)S(1)} %select_reduce_fusion.2) | copy-start | bytes 12292
  258.7 19.6 %copy-start.12 = (f32[1024,768]{0,1:T(8,128)S(1)}, f32[1024,768]{0,1:T(8,128)}, u32[]{:S(2)}) copy-start(f32[1024,768]{0,1:T(8,128)} %copy-done.11) | copy-start | bytes 9437188
  296.1 9.5 %copy-start.1 = (bf16[2,512,12,64]{1,3,2,0:T(8,128)(2,1)S(1)}, bf16[2,512,12,64]{1,3,2,0:T(8,128)(2,1)}, u32[]{:S(2)}) copy-start(bf16[2,512,12,64]{1,3,2,0:T(8,128)(2,1)} %copy-done) | copy-start | bytes 4718596
  296.1 9.5 %copy-start.4 = (bf16[2,512,12,64]{1,3,2,0:T(8,128)(2,1)S(1)}, bf16[2,512,12,64]{1,3,2,0:T(8,128)(2,1)}, u32[]{:S(2)}) copy-start(bf16[2,512,12,64]{1,3,2,0:T(8,128)(2,1)} %copy-done.3) | copy-start | bytes 4718596
  296.1 9.5 %copy-start.28 = (f32[2,12,512,1]{2,1,3,0:T(8,128)S(1)}, f32[2,12,512,1]{2,1,3,0:T(8,128)}, u32[]{:S(2)}) copy-start(f32[2,12,512,1]{2,1,3,0:T(8,128)} %copy-done.27) | copy-start | bytes 147460
  388.4 248.7 %reduce-scatter.5.cloned.1.call-start = ((), (), s32[]{:S(2)}) async-start(), calls=%async_computation.7 | async-start | bytes 10137600 | tf_op jit(solution)/shard_map/reduce_scatter | solution.py:288
  443.4 9.0 %copy-start.46 = (f32[256]{0:T(256)S(1)}, f32[256]{0:T(256)}, u32[]{:S(2)}) copy-start(f32[256]{0:T(256)} %copy-done.45) | copy-start | bytes 3076
  443.4 9.0 %copy-start.48 = (f32[256]{0:T(256)S(1)}, f32[256]{0:T(256)}, u32[]{:S(2)}) copy-start(f32[256]{0:T(256)} %copy-done.47) | copy-start | bytes 3076
  449.8 10.1 %all-to-all-start.2 = ((f32[32,3,128]{2,1,0:T(4,128)}), f32[32,3,128]{2,1,0:T(4,128)S(1)}, u32[]{:S(2)}, u32[]{:S(2)}) async-start(f32[32,3,128]{2,1,0:T(4,128)} %reshape.399), calls=%async_computation.3 | async-start | bytes 131072 | tf_op jit(solution)/shard_map/all_to_all | solution.py:44
  (47 other events, 129.9 us)
Sparse Core Ops, SparseCore 0:
  10.8 63.5 all-gather.4
  77.3 87.6 all-gather.6
  388.5 104.8 reduce-scatter.2
  500.2 136.8 reduce-scatter.4

commit v2 on v0

v2 whole, which is shorter than its diff:
```python
import functools, math
import jax, jax.numpy as jnp
from jax import lax
from jax.experimental import pallas as pl
from jax.experimental.pallas import tpu as pltpu
from jax.sharding import PartitionSpec as P
PACK=512; SEGS_PACK=4; HEADS=12; HEAD_DIM=64; LANES=128
MASKED=-1e30
VMEM_MOST=60*1024*1024
F32=jnp.float32; BF16=jnp.bfloat16
def dot_nn(a,b): return jnp.dot(a,b,preferred_element_type=F32)
def dot_nt(a,b): return lax.dot_general(a,b,(((1,),(1,)),((),())),preferred_element_type=F32)
def dot_tn(a,b): return lax.dot_general(a,b,(((0,),(0,)),((),())),preferred_element_type=F32)

def segment_tiles(lens_ref, g):
    row=lax.broadcasted_iota(jnp.int32,(PACK,LANES),0)
    lane=lax.broadcasted_iota(jnp.int32,(PACK,LANES),1)
    seg=jnp.zeros((PACK,LANES),jnp.int32); bound=jnp.int32(0)
    for j in range(SEGS_PACK):
        bound=bound+lens_ref[g,j]
        seg=seg+(row>=bound).astype(jnp.int32)
    place=lane-48
    inside=jnp.logical_and(place>=0,place<SEGS_PACK)
    same=place==seg
    apart=jnp.where(jnp.logical_and(inside,jnp.logical_not(same)),MASKED,0.0)
    own=jnp.where(same,1.0,0.0)
    return lane,apart,own

def head_lanes(lane,h):
    return jnp.logical_and(lane<48,lane%16==h)

def attention_kernel(lens_ref,tok_ref,w_ref,b_ref,mix_ref,ctx_ref,lse_ref,acc_ref):
    g=pl.program_id(0)
    wide=w_ref.shape[1]; width=wide//3
    lane,apart,own=segment_tiles(lens_ref,g)
    apart=apart.astype(BF16); own=own.astype(BF16)
    tok=tok_ref[...]
    mix_ref[:,:width]=((dot_nn(tok,w_ref[:,:width])+b_ref[:,:width]).astype(BF16).astype(F32)*(1/math.sqrt(HEAD_DIM))).astype(BF16)
    mix_ref[:,width:2*width]=(dot_nn(tok,w_ref[:,width:2*width])+b_ref[:,width:2*width]).astype(BF16)
    mix_ref[:,2*width:]=(dot_nn(tok,w_ref[:,2*width:])+b_ref[:,2*width:]).astype(BF16)
    acc_ref[...]=jnp.zeros_like(acc_ref)
    ones=jnp.ones((PACK,LANES),BF16)
    def pair(p,carry):
        at=lambda base: pl.ds(pl.multiple_of(base+p*LANES,LANES),LANES)
        q2=mix_ref[:,at(0)]; k2=mix_ref[:,at(width)]; v2=mix_ref[:,at(2*width)]
        kx=jnp.concatenate([k2,own],axis=1)
        vx=jnp.concatenate([v2,ones],axis=1)
        outs=[]
        for half in range(2):
            qm=jnp.where(lane//HEAD_DIM==half,q2,jnp.zeros_like(q2))
            s=dot_nt(jnp.concatenate([qm,apart],axis=1),kx)
            m=jnp.max(s,axis=1,keepdims=True)
            w=jnp.exp(s-m).astype(BF16)
            o=dot_nn(w,vx)
            total=o[:,LANES:]
            outs.append(o[:,:LANES]/total)
            acc_ref[...]=jnp.where(head_lanes(lane,2*p+half),m+jnp.log(total),acc_ref[...])
        ctx_ref[:,at(0)]=jnp.where(lane<HEAD_DIM,outs[0],outs[1]).astype(BF16)
        return carry
    lax.fori_loop(0,HEADS//2,pair,0)
    lse_ref[...]=acc_ref[...]

def attention(lens,tok,w,b):
    rows,width=tok.shape; wide=w.shape[1]
    return pl.pallas_call(attention_kernel,grid=(rows//PACK,),
        in_specs=[pl.BlockSpec(memory_space=pltpu.SMEM),pl.BlockSpec((PACK,width),lambda g:(g,0)),
                  pl.BlockSpec(w.shape,lambda g:(0,0)),pl.BlockSpec((1,wide),lambda g:(0,0))],
        out_specs=[pl.BlockSpec((PACK,wide),lambda g:(g,0)),pl.BlockSpec((PACK,width),lambda g:(g,0)),pl.BlockSpec((PACK,LANES),lambda g:(g,0))],
        out_shape=[jax.ShapeDtypeStruct((rows,wide),BF16),jax.ShapeDtypeStruct((rows,width),BF16),jax.ShapeDtypeStruct((rows,LANES),F32)],
        scratch_shapes=[pltpu.VMEM((PACK,LANES),F32)],
        compiler_params=pltpu.CompilerParams(vmem_limit_bytes=VMEM_MOST),name='attention')(lens,tok,w,b)

def split_three(x,lane):
    hi=x.astype(BF16).astype(F32)
    rest=x-hi
    mid=rest.astype(BF16).astype(F32)
    return jnp.where(lane<16,hi,jnp.where(lane<32,mid,jnp.where(lane<48,rest-mid,0.0)))

def attention_grad_kernel(lens_ref,mix_ref,ctx_ref,dctx_ref,lse_ref,out_ref):
    g=pl.program_id(0)
    width=ctx_ref.shape[1]
    lane,apart,own=segment_tiles(lens_ref,g)
    prod=dctx_ref[...].astype(F32)*ctx_ref[...].astype(F32)
    hi=prod.astype(BF16); lo=(prod-hi.astype(F32)).astype(BF16)
    wr=lax.broadcasted_iota(jnp.int32,(width,LANES),0); wl=lax.broadcasted_iota(jnp.int32,(width,LANES),1)
    pick=jnp.where(jnp.logical_and(wl<48,wl%16==wr//HEAD_DIM),1.0,0.0).astype(BF16)
    dots=dot_nn(hi,pick)+dot_nn(lo,pick)
    qe=(apart-split_three(lse_ref[...],lane)).astype(BF16)
    de=(-split_three(dots,lane)).astype(BF16)
    def pair(p,carry):
        at=lambda base: pl.ds(pl.multiple_of(base+p*LANES,LANES),LANES)
        q2=mix_ref[:,at(0)]; k2=mix_ref[:,at(width)]; v2=mix_ref[:,at(2*width)]; d2=dctx_ref[:,at(0)]
        kt=k2.T
        dk=jnp.zeros((PACK,LANES),F32); dv=jnp.zeros((PACK,LANES),F32); dqs=[]
        for half in range(2):
            here=lane//HEAD_DIM==half
            qm=jnp.where(here,q2,jnp.zeros_like(q2)); dm=jnp.where(here,d2,jnp.zeros_like(d2))
            mark=jnp.where(head_lanes(lane,2*p+half),1.0,0.0)
            kx=jnp.concatenate([k2,(own+mark).astype(BF16)],axis=1)
            vx=jnp.concatenate([v2,mark.astype(BF16)],axis=1)
            st=dot_nt(kx,jnp.concatenate([qm,qe],axis=1))
            pt=jnp.exp(st)
            dpt=dot_nt(vx,jnp.concatenate([dm,de],axis=1))
            ds=(pt*dpt).astype(BF16)
            dv=dv+dot_nn(pt.astype(BF16),dm)
            dk=dk+dot_nn(ds,qm)
            dqs.append(dot_nn(kt[half*HEAD_DIM:(half+1)*HEAD_DIM],ds))
        dq=jnp.concatenate(dqs,axis=0).T*(1/math.sqrt(HEAD_DIM))
        out_ref[:,at(0)]=dq.astype(BF16)
        out_ref[:,at(width)]=dk.astype(BF16)
        out_ref[:,at(2*width)]=dv.astype(BF16)
        return carry
    lax.fori_loop(0,HEADS//2,pair,0)

def attention_grad(lens,mix,ctx,dctx,lse):
    rows,width=ctx.shape; wide=mix.shape[1]
    b=lambda n: pl.BlockSpec((PACK,n),lambda g:(g,0))
    return pl.pallas_call(attention_grad_kernel,grid=(rows//PACK,),
        in_specs=[pl.BlockSpec(memory_space=pltpu.SMEM),b(wide),b(width),b(width),b(LANES)],
        out_specs=b(wide),out_shape=jax.ShapeDtypeStruct((rows,wide),BF16),
        compiler_params=pltpu.CompilerParams(vmem_limit_bytes=VMEM_MOST),name='attention_grad')(lens,mix,ctx,dctx,lse)
EPS=1e-6
TILE=256
def half_tail(a, e):
    t=1.0/(1.0+0.3275911*a)
    p=t*(0.5*0.254829592+t*(0.5*-0.284496736+t*(0.5*1.421413741+t*(0.5*-1.453152027+t*(0.5*1.061405429)))))
    return p*e

def gelu_pair(x):
    z=jnp.abs(x)*(1/math.sqrt(2))
    e=jnp.exp(-z*z)
    h=half_tail(z,e)
    phi=jnp.where(x>0,1.0-h,h)
    return x*phi, phi+x*(e*(1/math.sqrt(2*math.pi)))

def normed(h):
    c=h-jnp.mean(h,axis=1,keepdims=True)
    f=lax.rsqrt(jnp.mean(c*c,axis=1,keepdims=True)+EPS)
    return c*f,f

def norm_back(e,n,f):
    return f*(e-jnp.mean(e,axis=1,keepdims=True)-n*jnp.mean(e*n,axis=1,keepdims=True))

def row_segments(lens_ref,first_row,rows):
    row=first_row+lax.broadcasted_iota(jnp.int32,(rows,LANES),0)
    lane=lax.broadcasted_iota(jnp.int32,(rows,LANES),1)
    packs=lens_ref.shape[0]
    seg=jnp.zeros((rows,LANES),jnp.int32)
    for g in range(packs):
        end=jnp.int32(g*PACK)
        for j in range(SEGS_PACK):
            end=end+lens_ref[g,j]
            seg=seg+(row>=end).astype(jnp.int32)
    return seg==lane

def feed_forward_kernel(lens_ref,ctx_ref,tok_ref,w_ref,vec_ref,n1_ref,r1_ref,low_ref,act_ref,dg_ref,n2_ref,r2_ref,res_ref,span_ref,score_ref,doc_ref,all_ref):
    i=pl.program_id(0)
    width=ctx_ref.shape[1]; rows=ctx_ref.shape[0]; reps=act_ref.shape[1]//width
    vec=lambda k: vec_ref[k:k+1,:]
    base=2*reps*width
    att=dot_nn(ctx_ref[...],w_ref[:,base:base+width])+vec(0)
    n1,f1=normed(tok_ref[...].astype(F32)+att)
    n1_ref[...]=n1; r1_ref[...]=jnp.broadcast_to(f1,(rows,LANES))
    first=n1*vec(1)+vec(2)
    low=first.astype(BF16); low_ref[...]=low
    out=first+vec(3)
    for q in range(reps):
        c=slice(q*width,(q+1)*width)
        x=dot_nn(low,w_ref[:,c])+vec(8+q)
        a,d=gelu_pair(x)
        a=a.astype(BF16)
        act_ref[:,c]=a; dg_ref[:,c]=d.astype(BF16)
        out=out+dot_nn(a,w_ref[:,(reps+q)*width:(reps+q+1)*width])
    n2,f2=normed(out)
    n2_ref[...]=n2; r2_ref[...]=jnp.broadcast_to(f2,(rows,LANES))
    res=(n2*vec(4)+vec(5)).astype(BF16)
    res_ref[...]=res
    span=dot_nn(res,w_ref[:,base+width:base+width+LANES])
    span_ref[...]=span
    score=jnp.broadcast_to(jnp.sum(span*vec_ref[6:7,:LANES],axis=1,keepdims=True),(rows,LANES))
    score_ref[...]=score
    all_ref[pl.ds(pl.multiple_of(i*rows,rows),rows),:]=score
    @pl.when(i==pl.num_programs(0)-1)
    def _():
        member=row_segments(lens_ref,0,all_ref.shape[0])
        s=jnp.where(member,all_ref[...],MASKED)
        top=jnp.max(s,axis=0,keepdims=True)
        total=jnp.sum(jnp.where(member,jnp.exp(s-top),0.0),axis=0,keepdims=True)
        real=lax.broadcasted_iota(jnp.int32,(1,LANES),1)<lens_ref.shape[0]*SEGS_PACK
        doc_ref[...]=jnp.where(real,top+jnp.log(jnp.where(real,total,1.0)),MASKED)

def once(shape):
    return pl.BlockSpec(shape,lambda i:(0,)*len(shape),pipeline_mode=pl.Buffered(1))

def feed_forward(lens,ctx,tok,w,vec,reps):
    rows,width=ctx.shape; ff=reps*width
    b=lambda n: pl.BlockSpec((TILE,n),lambda i:(i,0))
    s=lambda n,t: jax.ShapeDtypeStruct((rows,n),t)
    return pl.pallas_call(feed_forward_kernel,grid=(rows//TILE,),
        in_specs=[pl.BlockSpec(memory_space=pltpu.SMEM),b(width),b(width),once(w.shape),once(vec.shape)],
        out_specs=[b(width),b(LANES),b(width),b(ff),b(ff),b(width),b(LANES),b(width),b(LANES),b(LANES),once((1,LANES))],
        out_shape=[s(width,F32),s(LANES,F32),s(width,BF16),s(ff,BF16),s(ff,BF16),s(width,F32),s(LANES,F32),s(width,BF16),s(LANES,F32),s(LANES,F32),jax.ShapeDtypeStruct((1,LANES),F32)],
        scratch_shapes=[pltpu.VMEM((rows,LANES),F32)],
        compiler_params=pltpu.CompilerParams(vmem_limit_bytes=VMEM_MOST),name='feed_forward')(lens,ctx,tok,w,vec)

def feed_forward_grad_kernel(lens_ref,own_ids_ref,doc_ref,scores_ref,ids_ref,cot_ref,n2_ref,r2_ref,res_ref,span_ref,score_ref,dg_ref,n1_ref,r1_ref,w_ref,vec_ref,
                   olow_ref,ilow_ref,alow_ref,fsum_ref,dctx_ref,small_ref,spanw_ref,weight_ref,acc_ref):
    i=pl.program_id(0); last=pl.num_programs(0)-1
    rows,width=cot_ref.shape; reps=dg_ref.shape[1]//width
    vec=lambda k: vec_ref[k:k+1,:]
    base=2*reps*width
    @pl.when(i==0)
    def _():
        lane=lax.broadcasted_iota(jnp.int32,(1,LANES),1)
        marg=jnp.zeros((1,LANES),F32)
        for s in range(own_ids_ref.shape[0]):
            hit=ids_ref[...]==own_ids_ref[s].astype(F32)
            x=jnp.where(hit,scores_ref[...],MASKED)
            top=jnp.max(jnp.max(x,axis=1,keepdims=True),axis=0,keepdims=True)
            total=jnp.where(hit,jnp.exp(x-top),0.0)
            total=jnp.sum(jnp.sum(total,axis=1,keepdims=True),axis=0,keepdims=True)
            marg=jnp.where(lane==s,top+jnp.log(total),marg)
        weight_ref[...]=jnp.exp(doc_ref[...]-marg)
        small_ref[...]=jnp.zeros_like(small_ref)
        acc_ref[...]=jnp.zeros_like(acc_ref)
    member=row_segments(lens_ref,i*rows,rows)
    part=jnp.where(member,jnp.exp(jnp.where(member,score_ref[...]-doc_ref[...],0.0))*weight_ref[...],0.0)
    tw=jnp.sum(part,axis=1,keepdims=True)
    ans=vec_ref[6:7,:LANES]
    small_ref[6:7,:LANES]+=jnp.sum(tw*span_ref[...],axis=0,keepdims=True)
    sg=(tw*ans).astype(BF16)
    acc_ref[...]+=dot_tn(res_ref[...],sg)
    @pl.when(i==last)
    def _():
        spanw_ref[...]=acc_ref[...].astype(BF16)
    rg=cot_ref[...].astype(F32)+dot_nt(sg,w_ref[:,base+width:base+width+LANES])
    n2=n2_ref[...]
    def colsum(k,v):
        small_ref[k:k+1,:]+=jnp.sum(v,axis=0,keepdims=True)
    colsum(0,rg*n2); colsum(1,rg)
    ssum=norm_back(rg*vec(4),n2,r2_ref[:,:1])
    olow=ssum.astype(BF16); olow_ref[...]=olow
    colsum(2,olow.astype(F32))
    fg=ssum
    for q in range(reps):
        c=slice(q*width,(q+1)*width)
        il=(dot_nt(olow,w_ref[:,(reps+q)*width:(reps+q+1)*width])*dg_ref[:,c].astype(F32)).astype(BF16)
        ilow_ref[:,c]=il
        colsum(8+q,il.astype(F32))
        fg=fg+dot_nt(il,w_ref[:,c])
    n1=n1_ref[...]
    colsum(3,fg*n1); colsum(4,fg)
    fsum=norm_back(fg*vec(1),n1,r1_ref[:,:1])
    fsum_ref[...]=fsum
    alow=fsum.astype(BF16); alow_ref[...]=alow
    colsum(5,alow.astype(F32))
    dctx_ref[...]=dot_nt(alow,w_ref[:,base:base+width]).astype(BF16)

def feed_forward_grad(lens,own_ids,doc,scores,ids,cot,n2,r2,res,span,score,dg,n1,r1,w,vec):
    rows,width=cot.shape; ff=dg.shape[1]
    b=lambda n: pl.BlockSpec((TILE,n),lambda i:(i,0))
    s=lambda n,t: jax.ShapeDtypeStruct((rows,n),t)
    sm=pl.BlockSpec(memory_space=pltpu.SMEM)
    return pl.pallas_call(feed_forward_grad_kernel,grid=(rows//TILE,),
        in_specs=[sm,sm,once(doc.shape),once(scores.shape),once(ids.shape),b(width),b(width),b(LANES),b(width),b(LANES),b(LANES),b(ff),b(width),b(LANES),once(w.shape),once(vec.shape)],
        out_specs=[b(width),b(ff),b(width),b(width),b(width),once(vec.shape),once((width,LANES))],
        out_shape=[s(width,BF16),s(ff,BF16),s(width,BF16),s(width,F32),s(width,BF16),jax.ShapeDtypeStruct(vec.shape,F32),jax.ShapeDtypeStruct((width,LANES),BF16)],
        scratch_shapes=[pltpu.VMEM((1,LANES),F32),pltpu.VMEM((width,LANES),F32)],
        compiler_params=pltpu.CompilerParams(vmem_limit_bytes=VMEM_MOST),name='feed_forward_grad')(lens,own_ids,doc,scores,ids,cot,n2,r2,res,span,score,dg,n1,r1,w,vec)

def early_kernel(reps,low_ref,ilow_ref,act_ref,olow_ref,ctx_ref,alow_ref,out_ref):
    j=pl.program_id(0)
    @pl.when(j<reps)
    def _(): out_ref[...]=dot_tn(low_ref[...],ilow_ref[...]).astype(BF16)
    @pl.when(jnp.logical_and(j>=reps,j<2*reps))
    def _(): out_ref[...]=dot_tn(act_ref[...],olow_ref[...]).astype(BF16)
    @pl.when(j==2*reps)
    def _(): out_ref[...]=dot_tn(ctx_ref[...],alow_ref[...]).astype(BF16)

def early_grads(low,ilow,act,olow,ctx,alow):
    rows,width=low.shape; reps=act.shape[1]//width
    full=once((rows,width))
    return pl.pallas_call(functools.partial(early_kernel,reps),grid=(2*reps+1,),
        in_specs=[full,pl.BlockSpec((rows,width),lambda j:(0,jnp.minimum(j,reps-1))),pl.BlockSpec((rows,width),lambda j:(0,jnp.clip(j-reps,0,reps-1))),full,full,full],
        out_specs=pl.BlockSpec((width,width),lambda j:(0,j)),out_shape=jax.ShapeDtypeStruct((width,(2*reps+1)*width),BF16),
        compiler_params=pltpu.CompilerParams(vmem_limit_bytes=VMEM_MOST),name='early_weight_grads')(low,ilow,act,olow,ctx,alow)

def late_kernel(tok_ref,mg_ref,out_ref,sum_ref):
    mg=mg_ref[...]
    out_ref[...]=dot_tn(tok_ref[...],mg).astype(BF16)
    sum_ref[...]=jnp.broadcast_to(jnp.sum(mg.astype(F32),axis=0,keepdims=True),sum_ref.shape)

def late_grads(tok,mg):
    rows,width=tok.shape; wide=mg.shape[1]
    return pl.pallas_call(late_kernel,grid=(wide//width,),
        in_specs=[once((rows,width)),pl.BlockSpec((rows,width),lambda j:(0,j))],
        out_specs=[pl.BlockSpec((width,width),lambda j:(0,j)),pl.BlockSpec((8,width),lambda j:(0,j))],
        out_shape=[jax.ShapeDtypeStruct((width,wide),BF16),jax.ShapeDtypeStruct((8,wide),F32)],
        compiler_params=pltpu.CompilerParams(vmem_limit_bytes=VMEM_MOST),name='late_weight_grads')(tok,mg)
AXES = ("dp", "fsdp")


def pack_lanes(parts):
    flat = jnp.concatenate(parts, axis=-1)
    wide = -(-flat.shape[-1] // LANES) * LANES
    flat = jnp.pad(flat, [(0, 0)] * (flat.ndim - 1) + [(0, wide - flat.shape[-1])])
    return flat.reshape(flat.shape[:-1] + (wide // LANES, LANES))


def unpack_lanes(packed, sizes):
    flat = packed.reshape(packed.shape[:-2] + (-1,))
    starts = [sum(sizes[:i]) for i in range(len(sizes))]
    return [flat[..., a : a + n] for a, n in zip(starts, sizes)]


def to_all(block, devices):
    return lax.all_to_all(jnp.broadcast_to(block[None], (devices,) + block.shape), AXES, 0, 0)


def shards(
    tokens,
    cotangent,
    doc_lengths,
    query_ids,
    qkv_weight,
    query_bias,
    value_bias,
    attn_weight,
    attn_bias,
    first_gain,
    first_shift,
    inner_weight,
    inner_bias,
    outer_weight,
    outer_bias,
    second_gain,
    second_shift,
    span_weight,
    answer_vector,
):
    rows, width = tokens.shape
    packs_here = rows // PACK
    devices = lax.axis_size("dp") * lax.axis_size("fsdp")
    share = qkv_weight.shape[0]
    ff = inner_weight.shape[1]
    reps = ff // width
    segs_here = packs_here * SEGS_PACK
    span = span_weight.shape[1]

    row_params = (attn_bias, first_gain, first_shift, outer_bias, second_gain, second_shift)
    smalls = row_params + (inner_bias, answer_vector, query_bias, value_bias)
    sizes = [v.shape[0] for v in smalls]
    id_row = jnp.pad(
        query_ids[:, 0].astype(F32)[None], ((0, 0), (0, LANES - segs_here)), constant_values=-1.0
    )
    packed = jnp.concatenate([pack_lanes([v.astype(F32) for v in smalls]), id_row], axis=0)
    small_all = to_all(packed, devices)
    ids_all = small_all[:, -1]
    columns = unpack_lanes(small_all[:, :-1], sizes)
    vectors = jnp.concatenate(
        [c.reshape(1, width) for c in columns[: len(row_params)]]
        + [
            jnp.pad(columns[-3].reshape(1, -1), ((0, 0), (0, width - span))),
            jnp.zeros((1, width), F32),
            columns[-4].reshape(devices, reps, share).transpose(1, 0, 2).reshape(reps, width),
        ],
        axis=0,
    )
    vectors = jnp.pad(vectors, ((0, -vectors.shape[0] % 8), (0, 0)))
    query_row = columns[-2].reshape(1, width)
    value_row = columns[-1].reshape(1, width)
    qkv_row = jnp.concatenate([query_row, jnp.zeros_like(query_row), value_row], axis=1)

    mix_full = lax.all_gather(qkv_weight, AXES, axis=0, tiled=True)
    inner_turned = (
        inner_weight.reshape(share, devices, reps, share).transpose(0, 2, 1, 3).reshape(share, ff)
    )
    outer_blocks = [outer_weight[q * share : (q + 1) * share] for q in range(reps)]
    rest = jnp.concatenate([inner_turned] + outer_blocks + [attn_weight, span_weight], axis=1)
    rest_full = lax.all_gather(rest, AXES, axis=0, tiled=True)

    mixed, context, logsum = attention(doc_lengths, tokens, mix_full, qkv_row)
    (
        normed_one,
        factor_one,
        first_low,
        active,
        gelu_slope,
        normed_two,
        factor_two,
        result,
        span_rows,
        token_score,
        doc_score,
    ) = feed_forward(doc_lengths, context, tokens, rest_full, vectors, reps)
    scores_all = to_all(doc_score, devices)[:, 0]

    outer_low, inner_low, attended_low, first_sum_grad, context_grad, small_sums, span_grad = (
        feed_forward_grad(
            doc_lengths,
            query_ids.reshape(-1),
            doc_score,
            scores_all,
            ids_all,
            cotangent,
            normed_two,
            factor_two,
            result,
            span_rows,
            token_score,
            gelu_slope,
            normed_one,
            factor_one,
            rest_full,
            vectors,
        )
    )
    early = early_grads(first_low, inner_low, active, outer_low, context, attended_low)
    early_own = lax.psum_scatter(early, "dp", scatter_dimension=0, tiled=True)
    early_own = lax.psum_scatter(early_own, "fsdp", scatter_dimension=0, tiled=True).astype(F32)

    mixed_grad = attention_grad(doc_lengths, mixed, context, context_grad, logsum)
    mix_grad, bias_sums = late_grads(tokens, mixed_grad)
    late = jnp.concatenate([mix_grad, span_grad], axis=1)
    late_own = lax.psum_scatter(late, AXES, scatter_dimension=0, tiled=True).astype(F32)
    input_grad = dot_nt(mixed_grad, mix_full) + first_sum_grad

    n_rows = small_sums.shape[0]
    by_owner = small_sums.reshape(n_rows, devices, share).transpose(1, 0, 2)
    biases = bias_sums[0].reshape(3, devices, share).transpose(1, 0, 2)
    small_grads = pack_lanes(
        [
            by_owner.reshape(devices, n_rows * share),
            biases.reshape(devices, 3 * share),
            small_sums[6, :span].reshape(devices, span // devices),
        ]
    )
    mine = jnp.sum(lax.all_to_all(small_grads, AXES, 0, 0), axis=0)
    own_rows, own_biases, answer_own = unpack_lanes(
        mine, [n_rows * share, 3 * share, span // devices]
    )
    row_of = lambda k: own_rows[k * share : (k + 1) * share]

    queries = lax.broadcasted_iota(F32, (packs_here * devices, 1), 0)
    member_query = ids_all[:, :segs_here].reshape(1, -1) == queries
    marginal = jax.nn.logsumexp(
        jnp.where(member_query, scores_all[:, :segs_here].reshape(1, -1), MASKED), axis=1
    )
    inner_own = (
        early_own[:, :ff].reshape(share, reps, devices, share).transpose(0, 2, 1, 3)
    ).reshape(share, ff)
    outer_own = jnp.concatenate(
        [early_own[:, ff + q * width : ff + (q + 1) * width] for q in range(reps)], axis=0
    )
    return (
        jnp.sum(marginal),
        result,
        input_grad,
        late_own[:, : 3 * width],
        own_biases[:share],
        own_biases[2 * share :],
        early_own[:, 2 * ff :],
        row_of(5),
        row_of(3),
        row_of(4),
        inner_own,
        own_rows[8 * share : (8 + reps) * share],
        outer_own,
        row_of(2),
        row_of(0),
        row_of(1),
        late_own[:, 3 * width :],
        answer_own,
    )


def solution(mesh):
    rows = P(AXES, None)
    flat = P(AXES)
    in_specs = (rows,) * 4 + (rows, flat, flat, rows, flat, flat, flat, rows, flat, rows)
    in_specs += (flat, flat, flat, rows, flat)
    out_specs = (P(), rows, rows, rows, flat, flat, rows, flat, flat, flat, rows, flat, rows)
    out_specs += (flat, flat, flat, rows, flat)
    return jax.shard_map(shards, mesh=mesh, in_specs=in_specs, out_specs=out_specs, check_vma=False)
```

time: 983 us -> 483 us (0.49)
  blocking collectives: 236 us -> 14.6 us
  matrix products: 191 us -> 8.27 us
  waiting for transfers between devices: 413 us -> 257 us
  Pallas kernels: 0 us -> 133 us
  local copies, waits for them, and re-layouts: 84.1 us -> 37.3 us
  other arithmetic: 37.7 us -> 9.55 us
    reduce_scatter x3 -> x2, waiting for transfers between devices: 283 us -> 69.9 us  [the longest x1 40 us: shards(): early_own = lax.psum_scatter(early, 'dp', scatter_dimension=0, tiled=True)]
    dot_general x31 -> x1, matrix products: 191 us -> 8.27 us  [dot_nt(): lax.dot_general(a, b, (((1,), (1,)), ((), ())), preferred_element_type=F32)]
    pallas_call x0 -> x6, Pallas kernels: none -> 133 us  [the longest x1 31.4 us: feed_forward(): pl.pallas_call(feed_forward_kernel, grid=(rows // TILE,), in_specs=[pl.Bl...]
    all_gather x4 -> x2, waiting for transfers between devices: 17.6 us -> 112 us  [the longest x1 68.1 us: shards(): rest_full = lax.all_gather(rest, AXES, axis=0, tiled=True)]
    unnamed x2 -> x0, blocking collectives: 84.5 us -> none
    all_gather x1 -> x0, blocking collectives: 72.8 us -> none  [shards(): lax.all_gather(span_weight, ('dp', 'fsdp'), axis=0, tiled=True)]
    unnamed x11 -> x6, waiting for transfers between devices: 112 us -> 68.7 us
    pmax x1 -> x0, blocking collectives: 39.6 us -> none  [shards(): peak_score = lax.pmax(local_peak, ('dp', 'fsdp'))]
  transfers between devices with their start and end apart: 9 -> 7, of which waited for: 4 -> 6; matrix products, arithmetic and copies ran while one was open for 29% -> 9% of each run, Pallas kernels for 0% -> 12%
where the time goes in v2:
time: 483 us; the launch traced here: 482 us
  waiting for transfers between devices  257 us (53%)
  Pallas kernels  133 us (28%)
  local copies, waits for them, and re-layouts  37.3 us (8%)
  blocking collectives  14.6 us (3%)
  between operations  14.3 us (3%)
  other arithmetic  9.55 us (2%)
  starting transfers between devices  8.47 us (2%)
  matrix products  8.27 us (2%)
    unnamed x6, waiting for transfers between devices  68.7 us
    all_gather x1, waiting for transfers between devices, shards(): rest_full = lax.all_gather(rest, AXES, axis=0, tiled=True)  68.1 us
    all_gather x1, waiting for transfers between devices, shards(): mix_full = lax.all_gather(qkv_weight, AXES, axis=0, tiled=True)  43.8 us
    reduce_scatter x1, waiting for transfers between devices, shards(): early_own = lax.psum_scatter(early, 'dp', scatter_dimension=0, tiled=True)  40 us
    pallas_call x1, Pallas kernels, feed_forward(): pl.pallas_call(feed_forward_kernel, grid=(rows // TILE,), in_specs=[pl.Bl...  31.4 us
    reduce_scatter x1, waiting for transfers between devices, shards(): lax.psum_scatter(early_own, 'fsdp', scatter_dimension=0, tiled=True)  29.9 us
    pallas_call x1, Pallas kernels, attention_grad(): pl.pallas_call(attention_grad_kernel, grid=(rows // PACK,), in_specs=[pl....  26.3 us
    pallas_call x1, Pallas kernels, feed_forward_grad(): pl.pallas_call(feed_forward_grad_kernel, grid=(rows // TILE,), in_specs=[...  25.6 us
  transfers between devices with their start and end apart: 7, of which 6 were waited for; matrix products, arithmetic and copies ran while one was open for 9% of the time, Pallas kernels for 12%

profile of v2, /device:TPU:0, one launch (start us, length us, event | category | flops | bytes accessed | tf_op | source)
XLA Modules:
  0.0 482.0 jit_solution(14748372115381360637)
XLA Ops:
  8.1 2.1 reshape.135
  12.8 14.6 %all_to_all.15 = f32[32,4,128]{2,1,0:T(4,128)S(1)} all-to-all(f32[32,4,128]{2,1,0:T(4,128)S(1)} %broadcast_in_dim.33), channel_id=1, replica_groups=mesh['dp'=8,'fsdp'=4] {'dp','fsdp'}, dimensions={0} | all-to-all | bytes 131072 | tf_op jit(solution)/shard_map/all_to_all | solution.py:317
  30.0 43.8 %all-gather.3.cloned.1.call-done.w_ref = bf16[768,2304]{1,0:T(8,128)(2,1)} async-done(((bf16[24,2304]{1,0:T(8,128)(2,1)}), bf16[768,2304]{1,0:T(8,128)(2,1)}) %all-gather.3.cloned.1.call-update) | async-done | bytes 3538960 | tf_op jit(solution)/shard_map/all_gather | solution.py:374
  73.9 22.2 %attention.1 = (bf16[1024,2304]{1,0:T(8,128)(2,1)}, bf16[1024,768]{1,0:T(8,128)(2,1)}, f32[1024,128]{1,0:T(8,128)}) custom-call(s32[2,4]{1,0:T(2,128)} %lens_ref.7, bf16[1024,768]{1,0:T(8,128)(2,1)} %tok_ref.5, bf16[768,2304]{1,0:T(8,128)(2,1)} %all-gather.3.cloned.1.call-done.w_ref, f32[1,2304]{1,0:T(1,128)} %pad_maximum_fusion.2.b_ref), custom_call_target="tpu_custom_call" | custom-call | tf_op jit(solution)/shard_map/attention/pallas_call | solution.py:65
  96.1 68.1 %all-gather.5.cloned.1.call-done.w_ref = bf16[768,7040]{1,0:T(8,128)(2,1)} async-done(((bf16[24,7040]{1,0:T(8,128)(2,1)}), bf16[768,7040]{1,0:T(8,128)(2,1)}) %all-gather.5.cloned.1.call-update) | async-done | bytes 10813456 | tf_op jit(solution)/shard_map/all_gather | solution.py:380
  164.2 31.4 %feed_forward.1 = (f32[1024,768]{1,0:T(8,128)}, f32[1024,128]{1,0:T(8,128)}, bf16[1024,768]{1,0:T(8,128)(2,1)}, bf16[1024,3072]{1,0:T(8,128)(2,1)}, bf16[1024,30...) custom-call(s32[2,4]{1,0:T(2,128)} %lens_ref.7, ...), custom_call_target="tpu_custom_call" | custom-call | tf_op jit(solution)/shard_map/feed_forward/pallas_call | solution.py:199
  196.9 3.1 all-to-all-start.1
  200.9 6.2 %all-to-all-done.1 = f32[32,1,128]{2,1,0:T(1,128)S(1)} async-done(((f32[32,1,128]{2,1,0:T(1,128)}), f32[32,1,128]{2,1,0:T(1,128)S(1)}, u32[]{:S(2)}, u32[]{:S(2)}) %all-to-all-start.1) | async-done | bytes 16416 | tf_op jit(solution)/shard_map/all_to_all | solution.py:317
  207.7 25.6 %feed_forward_grad.1 = (bf16[1024,768]{1,0:T(8,128)(2,1)}, bf16[1024,3072]{1,0:T(8,128)(2,1)}, bf16[1024,768]{1,0:T(8,128)(2,1)}, f32[1024,768]{1,0:T(8,128)}, b...) custom-call(s32[2,4]{1,0:T(2,128)} %lens_ref.7, s32[8]{0:T(128)} %bitcast.48, ...), custom_call_target="tpu_custom_call" | custom-call | tf_op jit(solution)/shard_map/feed_forward_grad/pallas_call | solution.py:264
  233.3 19.4 %early_weight_grads.1 = bf16[768,6912]{1,0:T(8,128)(2,1)} custom-call(bf16[1024,768]{1,0:T(8,128)(2,1)} %get-tuple-element.59.low_ref, bf16[1024,3072]{1,0:T(8,128)(2,1)} %get-tuple-element.60.ilow_ref, bf16[1024,3072]{1,0:T(8,128)(2,1)} %get-tuple-element.61.act_ref, bf16[1024,768]{1,0:T(8,128)(2,1)} %get-tuple-element.62.olow_ref, ...), custom_call_target="tpu_custom_call" | custom-call | tf_op jit(solution)/shard_map/early_weight_grads/pallas_call | solution.py:283
  252.7 26.3 %attention_grad.1.mg_ref = bf16[1024,2304]{1,0:T(8,128)(2,1)} custom-call(s32[2,4]{1,0:T(2,128)} %lens_ref.7, bf16[1024,2304]{1,0:T(8,128)(2,1)} %get-tuple-element.44.mix_ref, bf16[1024,768]{1,0:T(8,128)(2,1)} %get-tuple-element.41.ctx_ref, bf16[1024,768]{1,0:T(8,128)(2,1)} %get-tuple-element.52.dctx_ref, f32[1024,128]{1,0:T(8,128)} %get-tuple-element.53.lse_ref), custom_call_target="tpu_custom_call" | custom-call | tf_op jit(solution)/shard_map/attention_grad/pallas_call | solution.py:118
  279.0 7.9 %late_weight_grads.1 = (bf16[768,2304]{1,0:T(8,128)(2,1)}, f32[8,2304]{1,0:T(8,128)}) custom-call(bf16[1024,768]{1,0:T(8,128)(2,1)} %tok_ref.5, bf16[1024,2304]{1,0:T(8,128)(2,1)} %attention_grad.1.mg_ref), custom_call_target="tpu_custom_call" | custom-call | tf_op jit(solution)/shard_map/late_weight_grads/pallas_call | solution.py:295
  286.9 4.1 pad_maximum_fusion
  291.4 40.0 %reduce-scatter.6.cloned.1.call-done = bf16[96,6912]{1,0:T(8,128)(2,1)} async-done(((bf16[768,6912]{1,0:T(8,128)(2,1)}), bf16[96,6912]{1,0:T(8,128)(2,1)}) %reduce-scatter.6.cloned.1.call-update) | async-done | bytes 1327120 | tf_op jit(solution)/shard_map/reduce_scatter | solution.py:419
  331.4 1.4 eq.15
  332.8 1.5 slice_reduce_fusion
  334.3 1.4 reshape_squeeze.6
  335.7 1.5 copy.58
  337.2 1.4 copy.59
  338.6 1.7 reshape.146
  340.3 1.8 copy.57
  342.1 1.7 reshape.147
  345.0 1.4 reshape_squeeze.7
  346.4 1.5 select_maximum_fusion
  348.0 1.5 reshape.149
  349.5 4.7 all-to-all-start.2
  355.7 8.3 %convolution_add_fusion = f32[1024,768]{1,0:T(8,128)} fusion(f32[1024,768]{1,0:T(8,128)} %get-tuple-element.54, bf16[1024,2304]{1,0:T(8,128)(2,1)} %attention_grad.1.mg_ref, bf16[768,2304]{1,0:T(8,128)(2,1)S(1)} %copy-done), kind=kOutput, calls=%fused_computation.1 | convolution fusion | flops 3624665088 | bytes 14548992 | tf_op jit(solution)/shard_map/dot_general | solution.py:12
  367.5 68.0 %reduce-scatter.10.cloned.1.call-done = bf16[24,2432]{1,0:T(8,128)(2,1)} async-done(((bf16[768,2432]{1,0:T(8,128)(2,1)}), bf16[24,2432]{1,0:T(8,128)(2,1)}) %reduce-scatter.10.cloned.1.call-update) | async-done | bytes 116752
  435.4 1.6 slice.177
  437.0 1.3 slice.184
  438.3 29.9 %reduce-scatter.8.cloned.1.call-done = bf16[24,6912]{1,0:T(8,128)(2,1)} async-done(((bf16[96,6912]{1,0:T(8,128)(2,1)}), bf16[24,6912]{1,0:T(8,128)(2,1)}) %reduce-scatter.8.cloned.1.call-update) | async-done | bytes 331792 | tf_op jit(solution)/shard_map/reduce_scatter | solution.py:420
  471.5 2.6 reshape.152
  (108 shorter events, 19.7 us)
Async XLA Ops:
  7.2 4.5 copy-start.6
  7.2 4.5 copy-start.7
  7.2 4.6 copy-start.8
  7.2 5.3 %copy-start.20 = (bf16[24]{0:T(256)(128)(2,1)S(1)}, bf16[24]{0:T(256)(128)(2,1)}, u32[]{:S(2)}) copy-start(bf16[24]{0:T(256)(128)(2,1)} %param.24) | copy-start | bytes 148
  7.2 5.3 %copy-start.21 = (bf16[24]{0:T(256)(128)(2,1)S(1)}, bf16[24]{0:T(256)(128)(2,1)}, u32[]{:S(2)}) copy-start(bf16[24]{0:T(256)(128)(2,1)} %param.25) | copy-start | bytes 148
  7.2 5.3 %copy-start.12 = (bf16[24]{0:T(256)(128)(2,1)S(1)}, bf16[24]{0:T(256)(128)(2,1)}, u32[]{:S(2)}) copy-start(bf16[24]{0:T(256)(128)(2,1)} %param.27) | copy-start | bytes 148
  7.3 5.3 %copy-start.13 = (bf16[24]{0:T(256)(128)(2,1)S(1)}, bf16[24]{0:T(256)(128)(2,1)}, u32[]{:S(2)}) copy-start(bf16[24]{0:T(256)(128)(2,1)} %param.28) | copy-start | bytes 148
  7.3 5.3 %copy-start.14 = (bf16[24]{0:T(256)(128)(2,1)S(1)}, bf16[24]{0:T(256)(128)(2,1)}, u32[]{:S(2)}) copy-start(bf16[24]{0:T(256)(128)(2,1)} %param.29) | copy-start | bytes 148
  7.3 5.3 %copy-start.18 = (bf16[96]{0:T(256)(128)(2,1)S(1)}, bf16[96]{0:T(256)(128)(2,1)}, u32[]{:S(2)}) copy-start(bf16[96]{0:T(256)(128)(2,1)} %param.31) | copy-start | bytes 580
  7.3 5.3 %copy-start.15 = (bf16[24]{0:T(256)(128)(2,1)S(1)}, bf16[24]{0:T(256)(128)(2,1)}, u32[]{:S(2)}) copy-start(bf16[24]{0:T(256)(128)(2,1)} %param.33) | copy-start | bytes 148
  7.3 5.3 %copy-start.16 = (bf16[24]{0:T(256)(128)(2,1)S(1)}, bf16[24]{0:T(256)(128)(2,1)}, u32[]{:S(2)}) copy-start(bf16[24]{0:T(256)(128)(2,1)} %param.34) | copy-start | bytes 148
  7.3 5.3 %copy-start.17 = (bf16[24]{0:T(256)(128)(2,1)S(1)}, bf16[24]{0:T(256)(128)(2,1)}, u32[]{:S(2)}) copy-start(bf16[24]{0:T(256)(128)(2,1)} %param.35) | copy-start | bytes 148
  7.3 5.3 %copy-start.19 = (bf16[4]{0:T(256)(128)(2,1)S(1)}, bf16[4]{0:T(256)(128)(2,1)}, u32[]{:S(2)}) copy-start(bf16[4]{0:T(256)(128)(2,1)} %param.37) | copy-start | bytes 28
  7.3 5.4 %copy-start.11 = (s32[8,1]{0,1:T(1,128)S(1)}, s32[8,1]{0,1:T(1,128)}, u32[]{:S(2)}) copy-start(s32[8,1]{0,1:T(1,128)} %param.22) | copy-start | bytes 100
  7.3 66.5 %all-gather.3.cloned.1.call-start = ((), (), s32[]{:S(2)}) async-start(), calls=%async_computation.6 | async-start | bytes 3649536 | tf_op jit(solution)/shard_map/all_gather | solution.py:374
  8.1 156.2 %all-gather.5.cloned.1.call-start = ((), (), s32[]{:S(2)}) async-start(), calls=%async_computation.7 | async-start | bytes 11151360 | tf_op jit(solution)/shard_map/all_gather | solution.py:380
  11.8 0.7 copy-start.2
  196.9 10.2 %all-to-all-start.1 = ((f32[32,1,128]{2,1,0:T(1,128)}), f32[32,1,128]{2,1,0:T(1,128)S(1)}, u32[]{:S(2)}, u32[]{:S(2)}) async-start(f32[32,1,128]{2,1,0:T(1,128)} %broadcast_in_dim.35), calls=%async_computation.1 | async-start | bytes 32768 | tf_op jit(solution)/shard_map/all_to_all | solution.py:317
  200.0 131.4 %reduce-scatter.6.cloned.1.call-start = ((), (), s32[]{:S(2)}) async-start(), calls=%async_computation.8 | async-start | bytes 11943936 | tf_op jit(solution)/shard_map/reduce_scatter | solution.py:419
  207.1 0.6 copy-start.4
  252.7 182.7 %reduce-scatter.10.cloned.1.call-start = ((), (), s32[]{:S(2)}) async-start(), calls=%async_computation.10 | async-start | bytes 3852288
  279.0 7.9 %copy-start.3 = (bf16[768,128]{1,0:T(8,128)(2,1)S(1)}, bf16[768,128]{1,0:T(8,128)(2,1)}, u32[]{:S(2)}) copy-start(bf16[768,128]{1,0:T(8,128)(2,1)} %get-tuple-element.56) | copy-start | bytes 589828
  291.1 63.1 %copy-start.5 = (f32[32,1,128]{2,1,0:T(1,128)S(1)}, f32[32,1,128]{2,1,0:T(1,128)}, u32[]{:S(2)}) copy-start(f32[32,1,128]{2,1,0:T(1,128)} %copy-done.4) | copy-start | bytes 49156
  291.1 64.6 %copy-start = (bf16[768,2304]{1,0:T(8,128)(2,1)S(1)}, bf16[768,2304]{1,0:T(8,128)(2,1)}, u32[]{:S(2)}) copy-start(bf16[768,2304]{1,0:T(8,128)(2,1)} %all-gather.3.cloned.1.call-done.w_ref) | copy-start | bytes 10616836
  291.1 177.1 %reduce-scatter.8.cloned.1.call-start = ((), (), s32[]{:S(2)}) async-start(), calls=%async_computation.9 | async-start | bytes 1658880 | tf_op jit(solution)/shard_map/reduce_scatter | solution.py:420
  349.5 15.3 %all-to-all-start.2 = ((f32[32,4,128]{2,1,0:T(4,128)}), f32[32,4,128]{2,1,0:T(4,128)}, u32[]{:S(2)}, u32[]{:S(2)}) async-start(f32[32,4,128]{2,1,0:T(4,128)} %reshape.149), calls=%async_computation.2 | async-start | bytes 131072 | tf_op jit(solution)/shard_map/all_to_all | solution.py:438
  355.7 8.3 %copy-start.9 = (f32[256]{0:T(256)S(1)}, f32[256]{0:T(256)}, u32[]{:S(2)}) copy-start(f32[256]{0:T(256)} %eq.15) | copy-start | bytes 3076
  355.7 8.3 %copy-start.10 = (f32[256]{0:T(256)S(1)}, f32[256]{0:T(256)}, u32[]{:S(2)}) copy-start(f32[256]{0:T(256)} %broadcast_in_dim.36) | copy-start | bytes 3076
  469.1 5.0 %copy-start.1 = (bf16[24,6912]{1,0:T(8,128)(2,1)S(1)}, bf16[24,6912]{1,0:T(8,128)(2,1)}, u32[]{:S(2)}) copy-start(bf16[24,6912]{1,0:T(8,128)(2,1)} %reduce-scatter.8.cloned.1.call-done) | copy-start | bytes 995332
Sparse Core Ops, SparseCore 0:
  11.0 62.8 all-gather.2
  77.3 86.8 all-gather.4
  252.8 78.5 reduce-scatter.5
  336.9 98.4 reduce-scatter.9
  437.6 30.6 reduce-scatter.7
